TPU v7x, 128 devices: a whole 4x4x4 slice. The times are simulated.
128 devices in a mesh: row: 8 (over z_hi, y), col: 16 (over z_lo, x, core).
Axes of the slice: x: 4, y: 4, z: 4 (z_hi: 2, z_lo: 2; z = z_hi * 2 + z_lo), core: 2. Of those that a mesh axis runs over, the one named last changes fastest.
Arguments:
- node_coords: float32 [3, 131072], P(None, ('row', 'col')), may hold values from -0.08 to 66.08, as said below
- tet_nodes: int32 [4, 864000], P(None, ('row', 'col')), may hold values from -1 to 1535, as said below
- bnd_nodes: int32 [55808], P(('row', 'col')), may hold values from -1 to 1023, as said below
- reaction: float32 [131072], P(('row', 'col')), may hold values from 0.05 to 0.5
- load: float32 [131072], P(('row', 'col')), may hold values from -8 to 8
- area_normal: float32 [3, 55808], P(None, ('row', 'col')), may hold values from -2 to 2
Outputs:
- solution: float32 [131072], P(('row', 'col'))
- demag_potential: float32 [55808], P(('row', 'col'))
Inputs may be any that keep to these rules, and one draw needn't show every extreme that they name: `tet_nodes`: own node n of a partition lies in its layer n // 256; layers run along the grain, partitions of a grain follow their col index. Each column lists the corners of one tetrahedron as indices into the partition's ghost-extended list (see the steps); each lattice cell of a grain is split into six tetrahedra around one of its main diagonals, the same on every partition that lists them; every tetrahedron of the grain that has an own node of the partition as a corner stands exactly once on that partition; -1 marks an empty column, all four entries then -1. Tetrahedra have volumes bounded away from zero. `bnd_nodes`: each own node on the surface of its grain stands in exactly one slot of its partition; other slots hold -1. The partitions at the two ends of a grain fill all 436 slots. `node_coords`: node positions of the grains' meshes.
All inputs are finite; a program needn't handle non-finite values.
Results may differ from a plain program's by a relative error of at most 0.0003.
Values sent between devices are 32-bit elements; how exact they have to be, the bound alone decides.
A program may use at most 128 MiB of HBM per device.

v0:
```python
import math

import jax
import jax.numpy as jnp
from jax import lax
from jax.sharding import PartitionSpec as P

QS = 16
ITERS = 3


def extended_2(x, sides, width):
    for axis, dim in sides:
        devices, length = (lax.axis_size(axis), x.shape[dim])
        up = [(i, (i + 1) % devices) for i in range(devices - 1)]
        down = [(j, i) for i, j in up]
        last = lax.slice_in_dim(x, length - width, length, axis=dim)
        leading = lax.slice_in_dim(x, 0, width, axis=dim)
        before = lax.ppermute(last, axis, up)
        after = lax.ppermute(leading, axis, down)
        x = jnp.concatenate([before, x, after], axis=dim)
    return x


def cross_product(left_vec, right_vec):
    return jnp.stack(
        [
            left_vec[1] * right_vec[2] - left_vec[2] * right_vec[1],
            left_vec[2] * right_vec[0] - left_vec[0] * right_vec[2],
            left_vec[0] * right_vec[1] - left_vec[1] * right_vec[0],
        ]
    )


def element_matrices(ext_coords, corners):
    present = corners[0] >= 0
    corner_ids = jnp.maximum(corners, 0)
    vertex_zero = ext_coords[:, corner_ids[0]]
    edge_one = ext_coords[:, corner_ids[1]] - vertex_zero
    edge_two = ext_coords[:, corner_ids[2]] - vertex_zero
    edge_three = ext_coords[:, corner_ids[3]] - vertex_zero
    normal_one = cross_product(edge_two, edge_three)
    normal_two = cross_product(edge_three, edge_one)
    normal_three = cross_product(edge_one, edge_two)
    normal_zero = -(normal_one + normal_two + normal_three)
    volume_six = jnp.sum(edge_one * normal_one, axis=0)
    safe_volume = jnp.abs(jnp.where(present, volume_six, 1.0))
    weights = jnp.where(present, 1.0 / (6.0 * safe_volume), 0.0)
    normals = jnp.stack([normal_zero, normal_one, normal_two, normal_three])
    stiffness = jnp.sum(normals[:, None] * normals[None, :], axis=2) * weights
    return (stiffness, corner_ids)


def assemble(values, corner_ids, ext_len, own_count):
    accumulated = (
        jnp.zeros((ext_len,), values.dtype).at[corner_ids.reshape(-1)].add(values.reshape(-1))
    )
    margin = (ext_len - own_count) // 2
    return accumulated[margin : margin + own_count]


def tile_sum(targets, sources):
    delta_x = targets[0][:, None] - sources[0][None, :]
    delta_y = targets[1][:, None] - sources[1][None, :]
    delta_z = targets[2][:, None] - sources[2][None, :]
    distance = delta_x * delta_x + delta_y * delta_y + delta_z * delta_z + 0.25
    numerator = (
        delta_x * sources[3][None, :]
        + delta_y * sources[4][None, :]
        + delta_z * sources[5][None, :]
    )
    inverse = lax.rsqrt(distance)
    return jnp.sum(numerator * inverse * inverse * inverse, axis=1) * (0.25 / math.pi)


def blocked_sum(targets, sources, width):
    columns = sources.shape[1]
    blocks = sources.reshape(6, columns // width, width).transpose(1, 0, 2)

    def scan_step(running, src_block):
        return (running + tile_sum(targets, src_block), None)

    running, unused = lax.scan(scan_step, jnp.zeros((targets.shape[1],), jnp.float32), blocks)
    return running


def local(node_coords, tet_nodes, bnd_nodes, reaction, load, area_normal):
    square = QS * QS
    own_count = load.shape[0]
    ext_len = own_count + 2 * square
    ext_coords = extended_2(node_coords, (("col", 1),), square)
    stiffness, corner_ids = element_matrices(ext_coords, tet_nodes)
    diag_terms = jnp.stack([stiffness[k, k] for k in range(4)])
    diagonal = reaction + assemble(diag_terms, corner_ids, ext_len, own_count)
    solution = jnp.zeros_like(load)
    residual = load
    precond = residual / diagonal
    direction = precond
    rz_now = lax.psum(jnp.sum(residual * precond), ("row", "col"))
    for iteration in range(ITERS):
        extended = extended_2(direction, (("col", 0),), square)
        products = jnp.sum(stiffness * extended[corner_ids][None], axis=1)
        image = reaction * direction + assemble(products, corner_ids, ext_len, own_count)
        curvature = lax.psum(jnp.sum(direction * image), ("row", "col"))
        step_size = rz_now / curvature
        solution = solution + step_size * direction
        residual = residual - step_size * image
        if iteration + 1 < ITERS:
            precond = residual / diagonal
            rz_next = lax.psum(jnp.sum(residual * precond), ("row", "col"))
            direction = precond + rz_next / rz_now * direction
            rz_now = rz_next
    slot_count = bnd_nodes.shape[0]
    live_mask = (bnd_nodes >= 0).astype(jnp.float32)
    slot_ids = jnp.maximum(bnd_nodes, 0)
    positions = node_coords[:, slot_ids] * live_mask[None, :]
    traces = solution[slot_ids] * live_mask
    weighted = area_normal * traces[None, :]
    sources = jnp.concatenate([positions, weighted], axis=0)
    row_sums = blocked_sum(
        positions, lax.all_gather(sources, ("row", "col"), axis=1, tiled=True), 8 * slot_count
    )
    demag_potential = live_mask * (-0.5 * traces + row_sums)
    return (solution, demag_potential)


def solution(mesh):
    placed = (
        P(None, ("row", "col")),
        P(None, ("row", "col")),
        P(("row", "col")),
        P(("row", "col")),
        P(("row", "col")),
        P(None, ("row", "col")),
    )
    return jax.shard_map(
        local,
        mesh=mesh,
        in_specs=placed,
        out_specs=(P(("row", "col")), P(("row", "col"))),
        check_vma=False,
    )
```

profile of v0, /device:TPU:24, one launch (start us, length us, event | category | flops | bytes accessed | tf_op | source)
XLA Modules:
  0.0 1901.6 jit_solution(17606528600907032549)
XLA Ops:
  7.9 1.7 collective-permute-start
  9.7 1.3 collective-permute-start.1
  11.0 0.9 broadcast_maximum_fusion
  11.9 1.0 compare_reduce_fusion
  15.0 13.5 gather_fusion.1
  28.5 13.5 gather_fusion
  42.0 13.4 gather_fusion.2
  55.5 13.5 gather_fusion.3
  69.0 4.6 subtract_bitcast_fusion.1
  73.6 6.0 multiply_subtract_fusion.8
  79.6 10.5 multiply_reduce_fusion
  90.2 11.1 multiply_subtract_fusion.5
  101.3 6.6 multiply_subtract_fusion.2
  108.0 3.6 maximum_bitcast_fusion
  111.6 7.2 maximum_bitcast_fusion.1
  118.8 1.0 copy-done.7
  119.9 9.2 fusion.14
  129.1 10.1 pad_maximum_fusion
  139.1 7.9 copy.129
  147.1 8.0 copy.130
  155.9 150.7 %scatter_custom_fusion = f32[1536]{0:T(1024)S(1)} fusion(s32[27000]{0:T(1024)S(1)} %fusion.15, f32[27000]{0:T(1024)S(1)} %reshape.409, f32[]{:T(128)} %constant.18.clone.1), kind=kCustom, calls=%fused_computation.122 | custom fusion | flops 27000 | bytes 6148 | tf_op jit(solution)/shard_map/scatter-add | solution.py:56
  306.6 4.6 collective-permute-start.2
  311.3 1.3 collective-permute-start.3
  312.6 2.8 collective-permute-done.3
  315.4 138.7 %gather_fusion.4 = f32[27000]{0:T(1024)S(1)} fusion(f32[1536]{0:T(1024)S(1)} %pad_maximum_fusion.4, s32[27648]{0:T(1024)S(1)} %pad_clamp_fusion), kind=kCustom, calls=%fused_computation.4 | custom fusion | bytes 324000 | tf_op jit(solution)/shard_map/gather | solution.py:102
  454.8 150.7 %scatter_custom_fusion.1 = f32[1536]{0:T(1024)S(1)} fusion(s32[27000]{0:T(1024)S(1)} %fusion.15, f32[27000]{0:T(1024)S(1)} %reshape.417, f32[]{:T(128)} %constant.18.clone.1), kind=kCustom, calls=%fused_computation.120 | custom fusion | flops 27000 | bytes 6148 | tf_op jit(solution)/shard_map/scatter-add | solution.py:56
  606.1 105.4 %all-reduce = (f32[]{:T(128)}, f32[]{:T(128)}) all-reduce(f32[]{:T(128)} %get-tuple-element.75, f32[]{:T(128)} %get-tuple-element.74), channel_id=1, replica_groups=mesh['row'=8,'col'=16] {'row','col'}, use_global_device_ids=true, to_apply=%region_4.5 | all-reduce | flops 2 | bytes 16 | tf_op jit(solution)/shard_map/psum | solution.py:99
  713.4 63.6 %psum.44 = f32[]{:T(128)} all-reduce(f32[]{:T(128)} %get-tuple-element.88), channel_id=1, replica_groups=mesh['row'=8,'col'=16] {'row','col'}, use_global_device_ids=true, to_apply=%region_10.11 | all-reduce | flops 1 | bytes 8 | tf_op jit(solution)/shard_map/psum | solution.py:110
  778.4 1.6 collective-permute-start.4
  780.0 1.3 collective-permute-start.5
  781.3 1.7 collective-permute-done.5
  783.0 138.6 %gather_fusion.5 = f32[27000]{0:T(1024)S(1)} fusion(f32[1536]{0:T(1024)S(1)} %pad_maximum_fusion.5, s32[27648]{0:T(1024)S(1)} %pad_clamp_fusion), kind=kCustom, calls=%fused_computation.5 | custom fusion | bytes 324000 | tf_op jit(solution)/shard_map/gather | solution.py:102
  922.2 150.7 %scatter_custom_fusion.2 = f32[1536]{0:T(1024)S(1)} fusion(s32[27000]{0:T(1024)S(1)} %fusion.15, f32[27000]{0:T(1024)S(1)} %reshape.425, f32[]{:T(128)} %constant.18.clone.1), kind=kCustom, calls=%fused_computation.118 | custom fusion | flops 27000 | bytes 6148 | tf_op jit(solution)/shard_map/scatter-add | solution.py:56
  1073.5 83.9 %psum.45 = f32[]{:T(128)} all-reduce(f32[]{:T(128)} %multiply_reduce_fusion.6), channel_id=1, replica_groups=mesh['row'=8,'col'=16] {'row','col'}, use_global_device_ids=true, to_apply=%region_14.15 | all-reduce | flops 1 | bytes 8 | tf_op jit(solution)/shard_map/psum | solution.py:104
  1159.3 62.6 %psum.46 = f32[]{:T(128)} all-reduce(f32[]{:T(128)} %multiply_reduce_fusion.5), channel_id=1, replica_groups=mesh['row'=8,'col'=16] {'row','col'}, use_global_device_ids=true, to_apply=%region_16.17 | all-reduce | flops 1 | bytes 8 | tf_op jit(solution)/shard_map/psum | solution.py:110
  1223.3 1.7 collective-permute-start.6
  1225.0 1.3 collective-permute-start.7
  1226.6 2.4 collective-permute-done.7
  1229.0 138.6 %gather_fusion.6 = f32[27000]{0:T(1024)S(1)} fusion(f32[1536]{0:T(1024)S(1)} %pad_maximum_fusion.6, s32[27648]{0:T(1024)S(1)} %pad_clamp_fusion), kind=kCustom, calls=%fused_computation.6 | custom fusion | bytes 324000 | tf_op jit(solution)/shard_map/gather | solution.py:102
  1368.2 150.7 %scatter_custom_fusion.3 = f32[1536]{0:T(1024)S(1)} fusion(s32[27000]{0:T(1024)S(1)} %fusion.15, f32[27000]{0:T(1024)S(1)} %reshape.433, f32[]{:T(128)} %constant.18.clone.1), kind=kCustom, calls=%fused_computation.116 | custom fusion | flops 27000 | bytes 6148 | tf_op jit(solution)/shard_map/scatter-add | solution.py:56
  1519.5 1.3 gather_fusion.8
  1520.8 84.1 %psum.47 = f32[]{:T(128)} all-reduce(f32[]{:T(128)} %fusion.21), channel_id=1, replica_groups=mesh['row'=8,'col'=16] {'row','col'}, use_global_device_ids=true, to_apply=%region_20.21 | all-reduce | flops 1 | bytes 8 | tf_op jit(solution)/shard_map/psum | solution.py:104
  1606.3 2.1 gather_fusion.7
  1609.4 190.6 %all-gather.3.cloned.1.call-done = f32[128,436,6]{1,2,0:T(8,128)} async-done(((f32[1,436,6]{1,2,0:T(8,128)}), f32[128,436,6]{1,2,0:T(8,128)}) %all-gather.3.cloned.1.call-update) | async-done | bytes 1339408 | tf_op jit(solution)/shard_map/all_gather | solution.py:121
  1799.9 2.5 copy.133
  1802.4 1.2 reshape.446
  1803.7 0.9 reshape.332
  1804.6 89.4 %while.11 = (s32[]{:T(128)}, f32[436]{0:T(512)S(1)}, f32[3,436]{1,0:T(4,128)S(1)}, f32[16,6,3488]{2,0,1:T(8,128)S(1)}, s32[]{:T(128)}, /*index=5*/s32[]{:T(128)}, s32[]{}, s32[]{}, s32[]{}, s32[]{}, /*index=10*/s32[]{}) while((s32[]{:T(128)}, f32[436]{0:T(512)S(1)}, f32[3,436]{1,0:T(4,128)S(1)}, f32[16,6,3488]{2,0,1:T(8,128)S(1)}, ...), condition=%wide.region_23.24_spmd.clone, body=%wide.region_21.23_spmd.clone.sunk | while | flops 27374704 | bytes 274011 | solution.py:83
  1804.9 5.3 fusion.44
  1810.5 5.3 fusion.44
  1816.0 5.3 fusion.44
  1821.6 5.3 fusion.44
  1827.2 5.3 fusion.44
  1832.8 5.3 fusion.44
  1838.4 5.3 fusion.44
  1844.0 5.3 fusion.44
  1849.6 5.3 fusion.44
  1855.1 5.3 fusion.44
  1860.7 5.3 fusion.44
  1866.3 5.3 fusion.44
  1871.9 5.3 fusion.44
  1877.5 5.3 fusion.44
  1883.1 5.3 fusion.44
  1888.7 5.3 fusion.44
  (133 shorter events, 14.5 us)
Async XLA Ops:
  7.2 1792.8 %all-gather.3.cloned.1.call-start = ((), (), s32[]{:S(2)}) async-start(), calls=%async_computation | async-start | bytes 2113536 | tf_op jit(solution)/shard_map/all_gather | solution.py:121
  7.9 6.0 collective-permute-start
  9.7 4.3 collective-permute-start.1
  73.6 6.1 copy-start.1
  90.2 11.1 copy-start.2
  101.3 6.6 copy-start.6
  107.9 3.6 copy-start.8
  111.6 7.2 copy-start.3
  111.6 7.2 copy-start.4
  111.6 7.2 copy-start.5
  111.6 8.3 copy-start.7
  147.1 159.5 %copy-start.9 = (f32[1024]{0:T(1024)S(1)}, f32[1024]{0:T(1024)}, u32[]{:S(2)}) copy-start(f32[1024]{0:T(1024)} %param.11) | copy-start | bytes 12292
  147.1 159.5 %copy-start.11 = (f32[1024]{0:T(1024)S(1)}, f32[1024]{0:T(1024)}, u32[]{:S(2)}) copy-start(f32[1024]{0:T(1024)} %param.12) | copy-start | bytes 12292
  306.6 6.0 collective-permute-start.2
  311.3 4.1 collective-permute-start.3
  778.4 2.9 collective-permute-start.4
  780.0 3.0 collective-permute-start.5
  783.0 376.3 %copy-start.13 = (s32[436]{0:T(512)S(1)}, s32[436]{0:T(512)}, u32[]{:S(2)}) copy-start(s32[436]{0:T(512)} %param.10) | copy-start | bytes 5236
  783.0 443.3 %copy-start.10 = (f32[3,1024]{1,0:T(4,128)S(1)}, f32[3,1024]{1,0:T(4,128)}, u32[]{:S(2)}) copy-start(f32[3,1024]{1,0:T(4,128)} %param.8) | copy-start | bytes 36868
  1223.3 3.3 collective-permute-start.6
  1225.0 4.0 collective-permute-start.7
  1367.6 241.1 %copy-start.12 = (f32[3,436]{1,0:T(4,128)S(1)}, f32[3,436]{1,0:T(4,128)}, u32[]{:S(2)}) copy-start(f32[3,436]{1,0:T(4,128)} %param.13) | copy-start | bytes 15700
  1606.3 197.4 %copy-start = (f32[1024]{0:T(1024)}, f32[1024]{0:T(1024)S(1)}, u32[]{:S(2)}) copy-start(f32[1024]{0:T(1024)S(1)} %multiply_add_fusion) | copy-start | bytes 12292
Sparse Core Ops, SparseCore 0:
  1609.5 190.4 all-gather.2
where the time goes:
time: 1910 us; the launch traced here: 1900 us
  other arithmetic  766 us (40%)
  local copies, waits for them, and re-layouts  502 us (26%)
  blocking collectives  400 us (21%)
  waiting for transfers between devices  198 us (10%)
  between operations  21.6 us (1%)
    scatter-add x4, other arithmetic, assemble(): jnp.zeros((ext_len,), values.dtype).at[corner_ids.reshape(-1)]  603 us
    gather x6, local copies, waits for them, and re-layouts, local(): products = jnp.sum(stiffness * extended[corner_ids][None], axis=1)  416 us
    all_gather x1, waiting for transfers between devices, local(): lax.all_gather(sources, ('row', 'col'), axis=1, tiled=True)  191 us
    psum x2, blocking collectives, local(): curvature = lax.psum(jnp.sum(direction * image), ('row', 'col'))  168 us
    psum x2, blocking collectives, local(): rz_next = lax.psum(jnp.sum(residual * precond), ('row', 'col'))  126 us
    psum x1, blocking collectives, local(): rz_now = lax.psum(jnp.sum(residual * precond), ('row', 'col'))  105 us
    reduce_sum x16, other arithmetic, tile_sum(): jnp.sum(numerator * inverse * inverse * inverse, axis=1) * (0.25 / math.pi)  84.6 us
  transfers between devices with their start and end apart: 9, of which 4 were waited for; matrix products, arithmetic and copies ran while one was open for 0% of the time, Pallas kernels for 0%

commit v1 on v0

v1 whole, which is shorter than its diff:
```python
import functools
import math

import jax
import jax.numpy as jnp
from jax import lax
from jax.experimental import pallas as pl
from jax.experimental.pallas import tpu as pltpu
from jax.sharding import PartitionSpec as P

ITERS = 3
LANES = 128
SLOTS = 512
F32 = jnp.float32
BF16 = jnp.bfloat16
MESH = pl.DeviceIdType.MESH
VMEM = pl.BlockSpec(memory_space=pltpu.VMEM)
CHUNK = 2048
PAIRS = [(a, b) for a in range(4) for b in range(a, 4)]


def place():
    row, col = lax.axis_index("row"), lax.axis_index("col")
    z_hi, y = row // 4, row % 4
    z_lo, g = col // 8, col % 8
    return row, col, z_hi, y, z_lo, g


def peers():
    row, col, z_hi, y, z_lo, g = place()
    out = [(row, z_lo * 8 + (g + j) % 8) for j in range(1, 8)]
    out += [(z_hi * 4 + (y + j) % 4, col) for j in range(1, 4)]
    z = z_hi * 2 + z_lo
    for j in range(1, 4):
        other = (z + j) % 4
        out.append(((other // 2) * 4 + y, (other % 2) * 8 + g))
    return out


def lane_pick(table, low):
    return jnp.take_along_axis(table, low, axis=1, mode="promise_in_bounds")


def pick(rows, ids):
    low = ids & (LANES - 1)
    high = ids >> 7
    out = jnp.zeros(ids.shape, F32)
    for r, row in enumerate(rows):
        out = jnp.where(high == r, lane_pick(row, low), out)
    return out


def pieces(v):
    one = v.astype(BF16).astype(F32)
    rest = v - one
    two = rest.astype(BF16).astype(F32)
    return one, two, rest - two


def cross(u, v):
    return (
        u[1] * v[2] - u[2] * v[1],
        u[2] * v[0] - u[0] * v[2],
        u[0] * v[1] - u[1] * v[0],
    )


def dot3(u, v):
    return u[0] * v[0] + u[1] * v[1] + u[2] * v[2]


def chain_kernel(
    tet_ref, nc_ref, bnd_ref, an_ref, rea_ref, load_ref,
    sol_ref, g_ref, t_ref,
    ids, ext_c, ext_v, onehot, spread, stiff, vals, slots,
    red_a, red_y, red_z,
    halo_s, halo_r, red_s, red_r, all_s, all_r,
):
    row, col, z_hi, y, z_lo, g = place()
    z = z_hi * 2 + z_lo
    others = peers()
    before, after = (row, (col + 15) % 16), (row, (col + 1) % 16)
    elems = tet_ref.shape[1]
    count = bnd_ref.shape[1]
    tet_rows = ids.shape[1]

    barrier = pltpu.get_barrier_semaphore()
    for who in others + [before, after]:
        pl.semaphore_signal(barrier, inc=1, device_id=who, device_id_type=MESH)

    def send(src, dst, ssem, rsem, who):
        copy = pltpu.make_async_remote_copy(
            src_ref=src, dst_ref=dst, send_sem=ssem, recv_sem=rsem,
            device_id=who, device_id_type=MESH,
        )
        copy.start()
        return copy

    def halo(buf, k):
        return [
            send(buf.at[pl.ds(2, 2)], buf.at[pl.ds(10, 2)], halo_s.at[k, 0], halo_r.at[k, 0], before),
            send(buf.at[pl.ds(8, 2)], buf.at[pl.ds(0, 2)], halo_s.at[k, 1], halo_r.at[k, 1], after),
        ]

    def gather_stage(buf, k, stage):
        if stage == 0:
            part, first, last = buf.at[z_hi, y, z_lo, g], 0, 7
        elif stage == 1:
            part, first, last = buf.at[z_hi, y, z_lo], 7, 10
        else:
            part, first, last = buf.at[z_hi, :, z_lo], 10, 13
        return [send(part, part, all_s.at[k, j], all_r.at[k, j], others[j]) for j in range(first, last)]

    def finish(copies):
        for copy in copies:
            copy.wait()

    def reduce_all(u, v, k):
        for buf, mine, size, first in ((red_a, g, 8, 0), (red_y, y, 4, 7), (red_z, z, 4, 10)):
            here = buf.at[k]
            here[mine, 0] = u
            here[mine, 1] = v
            part = here.at[mine]
            finish([
                send(part, part, red_s.at[k, first + j], red_r.at[k, first + j], others[first + j])
                for j in range(size - 1)
            ])
            u, v = here[0, 0], here[0, 1]
            for i in range(1, size):
                u, v = u + here[i, 0], v + here[i, 1]
        return jnp.sum(u, keepdims=True), jnp.sum(v, keepdims=True)

    for s in range(8):
        for k in range(3):
            ext_c[2 + s, pl.ds(k, 1), :] = nc_ref[pl.ds(k, 1), pl.ds(s * LANES, LANES)]
        ext_c[2 + s, pl.ds(3, 5), :] = jnp.zeros((5, LANES), F32)

    slots[...] = jnp.full(slots.shape, -1, jnp.int32)
    for j in range(SLOTS // LANES):
        width = min(LANES, count - j * LANES)
        slots[pl.ds(j, 1), pl.ds(0, width)] = bnd_ref[:, pl.ds(j * LANES, width)]
    slot_ids = slots[...]
    live = jnp.where(slot_ids >= 0, 1.0, 0.0)
    mine = g_ref.at[z_hi, y, z_lo, g]
    mine[...] = jnp.zeros((8, SLOTS), F32)
    for k in range(3):
        tables = [jnp.broadcast_to(ext_c[2 + s, pl.ds(k, 1), :], (8, LANES)) for s in range(8)]
        spot = pick(tables, slot_ids)
        for j in range(SLOTS // LANES):
            mine[pl.ds(k, 1), pl.ds(j * LANES, LANES)] = spot[j : j + 1, :]
        mine[pl.ds(3 + k, 1), pl.ds(0, count)] = an_ref[pl.ds(k, 1), :]
    for j in range(SLOTS // LANES):
        mine[pl.ds(6, 1), pl.ds(j * LANES, LANES)] = live[j : j + 1, :]

    pl.semaphore_wait(barrier, len(others) + 2)
    coords_sent = halo(ext_c, 0)
    static_sent = gather_stage(g_ref, 0, 0)

    full = elems // LANES
    for a in range(4):
        ids[a, pl.ds(full // 8 * 8, tet_rows - full // 8 * 8), :] = jnp.full(
            (tet_rows - full // 8 * 8, LANES), -1, jnp.int32)
        for j in range(full):
            ids[a, pl.ds(j, 1), :] = tet_ref[pl.ds(a, 1), pl.ds(j * LANES, LANES)]
        rest = elems - full * LANES
        if rest:
            ids[a, pl.ds(full, 1), pl.ds(0, rest)] = tet_ref[pl.ds(a, 1), pl.ds(full * LANES, rest)]

    def build(q, carry):
        lane = lax.broadcasted_iota(jnp.int32, (LANES, LANES), 0)
        for a in range(4):
            low = jnp.broadcast_to(ids[a, pl.ds(q, 1), :] & (LANES - 1), (LANES, LANES))
            hot = jnp.where(low == lane, 1.0, 0.0).astype(BF16)
            onehot[:, pl.ds(pl.multiple_of((q * 4 + a) * LANES, LANES), LANES)] = hot
        return carry

    lax.fori_loop(0, tet_rows, build, 0)

    def node_sums():
        def spread_rows(q, carry):
            level = lax.broadcasted_iota(jnp.int32, (8, LANES), 0) + 2
            for a in range(4):
                high = jnp.broadcast_to(ids[a, pl.ds(q, 1), :] >> 7, (8, LANES))
                val = jnp.broadcast_to(vals[a, pl.ds(q, 1), :], (8, LANES))
                one, two, three = pieces(jnp.where(high == level, val, 0.0))
                block = jnp.concatenate([one, two, three, jnp.zeros((8, LANES), F32)], axis=0)
                spread[:, pl.ds(pl.multiple_of((q * 4 + a) * LANES, LANES), LANES)] = block.astype(BF16)
            return carry

        lax.fori_loop(0, tet_rows, spread_rows, 0)

        def accumulate(i, total):
            at = pl.ds(pl.multiple_of(i * CHUNK, CHUNK), CHUNK)
            return total + lax.dot_general(
                spread[:, at], onehot[:, at], (((1,), (1,)), ((), ())), preferred_element_type=F32)

        total = lax.fori_loop(0, onehot.shape[1] // CHUNK, accumulate, jnp.zeros((32, LANES), F32))
        return total[0:8] + total[8:16] + total[16:24]

    finish(coords_sent)
    finish(static_sent)
    static_sent = gather_stage(g_ref, 0, 1)

    def shape_elements(i, carry):
        at = pl.ds(pl.multiple_of(i * 8, 8), 8)
        corner = [ids[a, at, :] for a in range(4)]
        spots = []
        for a in range(4):
            low, high = corner[a] & (LANES - 1), corner[a] >> 7
            xyz = [jnp.zeros((8, LANES), F32) for _ in range(3)]
            for r in range(12):
                hit = high == r
                for k in range(3):
                    line = jnp.broadcast_to(ext_c[r, pl.ds(k, 1), :], (8, LANES))
                    xyz[k] = jnp.where(hit, lane_pick(line, low), xyz[k])
            spots.append(xyz)
        edges = [[spots[a][k] - spots[0][k] for k in range(3)] for a in range(1, 4)]
        n1 = cross(edges[1], edges[2])
        n2 = cross(edges[2], edges[0])
        n3 = cross(edges[0], edges[1])
        n0 = tuple(-(n1[k] + n2[k] + n3[k]) for k in range(3))
        present = corner[0] >= 0
        volume = jnp.abs(jnp.where(present, dot3(edges[0], n1), 1.0))
        weight = jnp.where(present, 1.0 / (6.0 * volume), 0.0)
        normals = (n0, n1, n2, n3)
        for e, (a, b) in enumerate(PAIRS):
            value = dot3(normals[a], normals[b]) * weight
            stiff[e, at, :] = value
            if a == b:
                vals[a, at, :] = value
        return carry

    lax.fori_loop(0, tet_rows // 8, shape_elements, 0)
    reaction = rea_ref[...]
    diagonal = reaction + node_sums()
    finish(static_sent)
    static_sent = gather_stage(g_ref, 0, 2)

    resid = load_ref[...]
    x = direction = image = gamma_old = alpha = None
    for k in range(ITERS):
        table = ext_v.at[k]
        precond = resid / diagonal
        for s in range(8):
            table[2 + s] = jnp.broadcast_to(precond[s : s + 1, :], (8, LANES))
        finish(halo(table, 1 + k))

        def products(i, carry):
            at = pl.ds(pl.multiple_of(i * 8, 8), 8)
            corner = []
            for a in range(4):
                corner.append(pick([table[r] for r in range(12)], ids[a, at, :]))
            sums = [None] * 4
            for e, (a, b) in enumerate(PAIRS):
                value = stiff[e, at, :]
                for m, n in {(a, b), (b, a)}:
                    term = value * corner[n]
                    sums[m] = term if sums[m] is None else sums[m] + term
            for a in range(4):
                vals[a, at, :] = sums[a]
            return carry

        lax.fori_loop(0, tet_rows // 8, products, 0)
        applied = reaction * precond + node_sums()
        gamma, delta = reduce_all(resid * precond, precond * applied, k)
        if k == 0:
            alpha = gamma / delta
            direction, image = precond, applied
            x = alpha * direction
        else:
            beta = gamma / gamma_old
            alpha = gamma / (delta - beta * gamma / alpha)
            direction = precond + beta * direction
            image = applied + beta * image
            x = x + alpha * direction
        if k + 1 < ITERS:
            resid = resid - alpha * image
        gamma_old = gamma

    sol_ref[...] = x
    tables = [jnp.broadcast_to(x[s : s + 1, :], (8, LANES)) for s in range(8)]
    t_ref[z_hi, y, z_lo, g] = pick(tables, slot_ids)
    finish(static_sent)
    for stage in range(3):
        finish(gather_stage(t_ref, 1, stage))


def pair_kernel(g_ref, t_ref, out_ref, lhs, acc, rows):
    row, col = lax.axis_index("row"), lax.axis_index("col")
    me = row * 16 + col
    count = out_ref.shape[1]
    padded = acc.shape[0]

    def trace_row(p):
        tile = t_ref[p]
        return jnp.concatenate([tile[j : j + 1, :] for j in range(SLOTS // LANES)], axis=1)

    own = g_ref[me]
    first = jnp.max(jnp.where(own[6:7] > 0, 1.0, 0.0) * own[0:3] + jnp.where(own[6:7] > 0, 0.0, -1e9), axis=1, keepdims=True)
    centre = jnp.concatenate([first, jnp.zeros((5, 1), F32)], axis=0)
    t = own[0:3] - first
    t_one, t_two, t_three = pieces(t)
    q_one, q_two, q_three = pieces(dot3((t[0:1], t[1:2], t[2:3]), (t[0:1], t[1:2], t[2:3])))
    none3 = jnp.zeros((3, SLOTS), F32)
    none1 = jnp.zeros((1, SLOTS), F32)
    unit = jnp.ones((1, SLOTS), F32)
    blocks_d, blocks_n = [], []
    for part, lead in ((t_one, 1), (t_two, 0), (t_three, 0), (t_one, 1), (t_two, 0), (t_one, 1)):
        flag = unit if lead else none1
        blocks_d += [-2.0 * part, none3, flag, none1]
        blocks_n += [none3, part, none1, -flag]
    blocks_d += [q_one, q_two, q_three] + [none1] * 13
    blocks_n += [none1] * 16
    fill = jnp.zeros((64, SLOTS), F32)
    for i, blocks in enumerate((blocks_d, blocks_n)):
        stacked = jnp.concatenate(blocks + [fill], axis=0)
        lhs[i] = stacked.T[0:padded, 0:64].astype(BF16)
    acc[...] = jnp.zeros_like(acc)
    rows[...] = jnp.zeros_like(rows)
    rows[pl.ds(48, 8), :] = jnp.where(lax.broadcasted_iota(jnp.int32, (8, SLOTS), 0) < 3, 1.0, 0.0).astype(F32)

    def step(p, carry):
        tile = g_ref[p]
        trace = trace_row(p)
        s = tile[0:3] - first
        w = tile[3:6] * trace
        sx, wx = [s[k : k + 1] for k in range(3)], [w[k : k + 1] for k in range(3)]
        data = jnp.concatenate([s, w, dot3(sx, sx) + 0.25, dot3(sx, wx)], axis=0)
        one, two, three = pieces(data)
        for i, part in enumerate((one, one, one, two, two, three)):
            rows[pl.ds(8 * i, 8), :] = part
        rhs = rows[...].astype(BF16)
        for m in range(0, padded, 64):
            d = jnp.dot(lhs[0, m : m + 64, :], rhs, preferred_element_type=F32)
            n = jnp.dot(lhs[1, m : m + 64, :], rhs, preferred_element_type=F32)
            inv = lax.rsqrt(d)
            c = (n * inv) * (inv * inv)
            acc[m : m + 64, :] += (c[:, 0:128] + c[:, 128:256]) + (c[:, 256:384] + c[:, 384:512])
        return carry

    lax.fori_loop(0, g_ref.shape[0], step, 0)
    sums = jnp.sum(acc[...].T, axis=0, keepdims=True) * (0.25 / math.pi)
    trace = trace_row(me)
    result = own[6:7, 0:padded] * (-0.5 * trace[:, 0:padded] + sums)
    out_ref[...] = result[:, 0:count]


def local(node_coords, tet_nodes, bnd_nodes, reaction, load, area_normal):
    elems, count = tet_nodes.shape[1], bnd_nodes.shape[0]
    tet_rows = -(-elems // 1024) * 8
    length = 4 * tet_rows * LANES
    sol, gathered, traces = pl.pallas_call(
        chain_kernel,
        out_shape=(
            jax.ShapeDtypeStruct((8, LANES), F32),
            jax.ShapeDtypeStruct((2, 4, 2, 8, 8, SLOTS), F32),
            jax.ShapeDtypeStruct((2, 4, 2, 8, 8, LANES), F32),
        ),
        in_specs=[VMEM] * 6,
        out_specs=(VMEM,) * 3,
        scratch_shapes=[
            pltpu.VMEM((4, tet_rows, LANES), jnp.int32),
            pltpu.VMEM((12, 8, LANES), F32),
            pltpu.VMEM((ITERS, 12, 8, LANES), F32),
            pltpu.VMEM((LANES, length), BF16),
            pltpu.VMEM((32, length), BF16),
            pltpu.VMEM((10, tet_rows, LANES), F32),
            pltpu.VMEM((4, tet_rows, LANES), F32),
            pltpu.VMEM((8, LANES), jnp.int32),
            pltpu.VMEM((ITERS, 8, 2, 8, LANES), F32),
            pltpu.VMEM((ITERS, 4, 2, 8, LANES), F32),
            pltpu.VMEM((ITERS, 4, 2, 8, LANES), F32),
            pltpu.SemaphoreType.DMA((1 + ITERS, 2)),
            pltpu.SemaphoreType.DMA((1 + ITERS, 2)),
            pltpu.SemaphoreType.DMA((ITERS, 13)),
            pltpu.SemaphoreType.DMA((ITERS, 13)),
            pltpu.SemaphoreType.DMA((2, 13)),
            pltpu.SemaphoreType.DMA((2, 13)),
        ],
        compiler_params=pltpu.CompilerParams(collective_id=0, has_side_effects=True, vmem_limit_bytes=60 << 20),
        name="chain",
    )(tet_nodes, node_coords, bnd_nodes.reshape(1, count), area_normal,
      reaction.reshape(8, LANES), load.reshape(8, LANES))
    padded = -(-count // 64) * 64
    demag = pl.pallas_call(
        pair_kernel,
        out_shape=jax.ShapeDtypeStruct((1, count), F32),
        in_specs=[VMEM] * 2,
        out_specs=VMEM,
        scratch_shapes=[
            pltpu.VMEM((2, padded, 64), BF16),
            pltpu.VMEM((padded, LANES), F32),
            pltpu.VMEM((64, SLOTS), F32),
        ],
        compiler_params=pltpu.CompilerParams(vmem_limit_bytes=60 << 20),
        name="pairs",
    )(gathered.reshape(128, 8, SLOTS), traces.reshape(128, 8, LANES))
    return sol.reshape(-1), demag.reshape(-1)


def solution(mesh):
    placed = (
        P(None, ("row", "col")),
        P(None, ("row", "col")),
        P(("row", "col")),
        P(("row", "col")),
        P(("row", "col")),
        P(None, ("row", "col")),
    )
    return jax.shard_map(
        local,
        mesh=mesh,
        in_specs=placed,
        out_specs=(P(("row", "col")), P(("row", "col"))),
        check_vma=False,
    )
```

time: 1910 us -> 158 us (0.08)
  other arithmetic: 766 us -> 0 us
  local copies, waits for them, and re-layouts: 502 us -> 0.6 us
  blocking collectives: 400 us -> 0 us
  waiting for transfers between devices: 198 us -> 0 us
  Pallas kernels: 0 us -> 155 us
  between operations: 21.6 us -> 0.65 us
    scatter-add x4 -> x0, other arithmetic: 603 us -> none  [assemble(): jnp.zeros((ext_len,), values.dtype).at[corner_ids.reshape(-1)]]
    gather x12 -> x0, local copies, waits for them, and re-layouts: 474 us -> none  [the longest x6 416 us: local(): products = jnp.sum(stiffness * extended[corner_ids][None], axis=1)]
    psum x5 -> x0, blocking collectives: 400 us -> none  [the longest x2 168 us: local(): curvature = lax.psum(jnp.sum(direction * image), ('row', 'col'))]
    all_gather x1 -> x0, waiting for transfers between devices: 191 us -> none  [local(): lax.all_gather(sources, ('row', 'col'), axis=1, tiled=True)]
    pallas_call x0 -> x2, Pallas kernels: none -> 155 us  [the longest x1 100 us: local(): pl.pallas_call(chain_kernel, out_shape=(jax.ShapeDtypeStruct((8, LANES),...]
    reduce_sum x26 -> x0, other arithmetic: 99.4 us -> none  [the longest x16 84.6 us: tile_sum(): jnp.sum(numerator * inverse * inverse * inverse, axis=1) * (0.25 / math.pi)]
    sub x4 -> x0, other arithmetic: 28.4 us -> none  [the longest x3 23.8 us: cross_product(): left_vec[1] * right_vec[2] - left_vec[2] * right_vec[1]]
    another operation x4 -> x0, other arithmetic: 21 us -> none  [the longest x3 20.9 us: element_matrices(): normals = jnp.stack([normal_zero, normal_one, normal_two, normal_three])]
  transfers between devices with their start and end apart: 9 -> 0, of which waited for: 4 -> 0; matrix products, arithmetic and copies ran while one was open for 0% -> 0% of each run, Pallas kernels for 0% -> 0%
where the time goes in v1:
time: 158 us; the launch traced here: 157 us
  Pallas kernels  155 us (98%)
    pallas_call x1, Pallas kernels, local(): pl.pallas_call(chain_kernel, out_shape=(jax.ShapeDtypeStruct((8, LANES),...  100 us
    pallas_call x1, Pallas kernels, local(): pl.pallas_call(pair_kernel, out_shape=jax.ShapeDtypeStruct((1, count), F3...  55.2 us

profile of v1, /device:TPU:24, one launch (start us, length us, event | category | flops | bytes accessed | tf_op | source)
XLA Modules:
  0.0 156.7 jit_solution(1234971278290845428)
XLA Ops:
  0.6 100.3 %chain.1 = (f32[8,128]{1,0:T(8,128)}, f32[2,4,2,8,8,512]{5,4,3,2,1,0:T(8,128)}, f32[2,4,2,8,8,128]{5,4,3,2,1,0:T(8,128)}) custom-call(s32[4,6750]{1,0:T(4,128)} %tet_ref.1, f32[3,1024]{1,0:T(4,128)} %nc_ref.1, s32[1,436]{1,0:T(1,128)} %bitcast.12, f32[3,436]{1,0:T(4,128)} %an_ref.1, f32[8,128]{1,0:T(8,128)} %bitcast.9, f32[8,128]{1,0:T(8,128)} %bitcast.10), custom_call_target="tpu_custom_call" | custom-call | tf_op jit(solution)/shard_map/chain/pallas_call | solution.py:352
  100.9 0.0 copy-start
  100.9 55.2 %pairs.1 = f32[1,436]{1,0:T(1,128)} custom-call(f32[128,8,512]{2,1,0:T(8,128)} %bitcast.7, f32[128,8,128]{2,1,0:T(8,128)} %bitcast.8), custom_call_target="tpu_custom_call" | custom-call | tf_op jit(solution)/shard_map/pairs/pallas_call | solution.py:385
  156.1 0.0 copy-done
  156.1 0.6 copy.9
Async XLA Ops:
  100.9 55.2 %copy-start = (f32[8,128]{1,0:T(8,128)S(1)}, f32[8,128]{1,0:T(8,128)}, u32[]{:S(2)}) copy-start(f32[8,128]{1,0:T(8,128)} %get-tuple-element.5) | copy-start | bytes 12292

commit v2 on v1

--- a/solution.py
+++ b/solution.py
@@ -16,6 +16,11 @@
 MESH = pl.DeviceIdType.MESH
 VMEM = pl.BlockSpec(memory_space=pltpu.VMEM)
 CHUNK = 2048
+QS = 16
+WIDE = 256
+MAIN = 4 * 4 * (QS - 1)
+BLOCK = 240
+UNROLL = 6
 PAIRS = [(a, b) for a in range(4) for b in range(a, 4)]
 
 
@@ -69,30 +74,50 @@
     return u[0] * v[0] + u[1] * v[1] + u[2] * v[2]
 
 
-def chain_kernel(
+def full_kernel(
     tet_ref, nc_ref, bnd_ref, an_ref, rea_ref, load_ref,
-    sol_ref, g_ref, t_ref,
-    ids, ext_c, ext_v, onehot, spread, stiff, vals, slots,
+    sol_ref, out_ref,
+    ids, ext_c, ext_v, onehot, spread, stiff, vals, slots, chosen, order,
+    source, trace, near, far, rhs, lhs, part, fin, fex,
     red_a, red_y, red_z,
-    halo_s, halo_r, red_s, red_r, all_s, all_r,
+    halo_s, halo_r, red_s, red_r, all_s, all_r, near_s, near_r, far_s, far_r,
+    fin_s, fin_r, fex_s, fex_r,
 ):
     row, col, z_hi, y, z_lo, g = place()
     z = z_hi * 2 + z_lo
     others = peers()
     before, after = (row, (col + 15) % 16), (row, (col + 1) % 16)
+    partner = (row, (1 - z_lo) * 8 + g)
+    column = [((row + j) % 8, col) for j in range(1, 8)]
+    keeper = (col % 8, (1 - col // 8) * 15)
+    at_end = col % 15 == 0
+    helped = row + (1 - col // 15) * 8
+    helpers = [(r, helped) for r in range(8)]
     elems = tet_ref.shape[1]
     count = bnd_ref.shape[1]
     tet_rows = ids.shape[1]
 
+    fex[...] = jnp.zeros(fex.shape, F32)
+    part[...] = jnp.zeros(part.shape, F32)
+
     barrier = pltpu.get_barrier_semaphore()
-    for who in others + [before, after]:
+    greeted = others + column + [before, after, keeper]
+    for who in greeted:
         pl.semaphore_signal(barrier, inc=1, device_id=who, device_id_type=MESH)
 
-    def send(src, dst, ssem, rsem, who):
-        copy = pltpu.make_async_remote_copy(
+    @pl.when(at_end)
+    def _():
+        for who in helpers:
+            pl.semaphore_signal(barrier, inc=1, device_id=who, device_id_type=MESH)
+
+    def remote(src, dst, ssem, rsem, who):
+        return pltpu.make_async_remote_copy(
             src_ref=src, dst_ref=dst, send_sem=ssem, recv_sem=rsem,
             device_id=who, device_id_type=MESH,
         )
+
+    def send(*args):
+        copy = remote(*args)
         copy.start()
         return copy
 
@@ -102,14 +127,13 @@
             send(buf.at[pl.ds(8, 2)], buf.at[pl.ds(0, 2)], halo_s.at[k, 1], halo_r.at[k, 1], after),
         ]
 
-    def gather_stage(buf, k, stage):
-        if stage == 0:
-            part, first, last = buf.at[z_hi, y, z_lo, g], 0, 7
-        elif stage == 1:
-            part, first, last = buf.at[z_hi, y, z_lo], 7, 10
-        else:
-            part, first, last = buf.at[z_hi, :, z_lo], 10, 13
-        return [send(part, part, all_s.at[k, j], all_r.at[k, j], others[j]) for j in range(first, last)]
+    def share(buf, k):
+        tile = buf.at[col]
+        return [send(tile, tile, all_s.at[k, j], all_r.at[k, j], others[j]) for j in range(7)]
+
+    def share_on(buf, k):
+        tiles = buf.at[pl.ds(z_lo * 8, 8)]
+        return [send(tiles, tiles, all_s.at[k, 7], all_r.at[k, 7], partner)]
 
     def finish(copies):
         for copy in copies:
@@ -120,9 +144,9 @@
             here = buf.at[k]
             here[mine, 0] = u
             here[mine, 1] = v
-            part = here.at[mine]
+            tile = here.at[mine]
             finish([
-                send(part, part, red_s.at[k, first + j], red_r.at[k, first + j], others[first + j])
+                send(tile, tile, red_s.at[k, first + j], red_r.at[k, first + j], others[first + j])
                 for j in range(size - 1)
             ])
             u, v = here[0, 0], here[0, 1]
@@ -141,20 +165,54 @@
         slots[pl.ds(j, 1), pl.ds(0, width)] = bnd_ref[:, pl.ds(j * LANES, width)]
     slot_ids = slots[...]
     live = jnp.where(slot_ids >= 0, 1.0, 0.0)
-    mine = g_ref.at[z_hi, y, z_lo, g]
-    mine[...] = jnp.zeros((8, SLOTS), F32)
+    tri = lax.broadcasted_iota(jnp.int32, (LANES, LANES), 0) <= lax.broadcasted_iota(jnp.int32, (LANES, LANES), 1)
+    tri = jnp.where(tri, 1.0, 0.0).astype(BF16)
+    rank = jnp.dot(live.astype(BF16), tri, preferred_element_type=F32) - 1.0
+    totals = jnp.sum(live, axis=1, keepdims=True)
+    base = jnp.zeros((1, 1), F32)
+    bases = []
+    for j in range(8):
+        bases.append(base)
+        base = base + totals[j : j + 1]
+    rank = rank + jnp.concatenate(bases, axis=0)
+    spot = (rank + jnp.where(rank >= MAIN, 1.0 * (WIDE - MAIN), 0.0)).astype(jnp.int32)
+    spot = jnp.where(slot_ids >= 0, spot, -1)
+    for j in range(SLOTS // LANES):
+        line = jnp.broadcast_to(spot[j : j + 1, :], (SLOTS, LANES))
+        hot = jnp.where(line == lax.broadcasted_iota(jnp.int32, (SLOTS, LANES), 0), 1.0, 0.0)
+        order[:, pl.ds(j * LANES, LANES)] = hot.astype(BF16)
+    tile = source.at[col]
+    tile[...] = jnp.zeros((8, SLOTS), F32)
+    for j in range(SLOTS // LANES):
+        tile[pl.ds(0, 1), pl.ds(j * LANES, LANES)] = (slot_ids[j : j + 1, :] + 1).astype(F32)
+    for k in range(3):
+        tile[pl.ds(1 + k, 1), pl.ds(0, count)] = an_ref[pl.ds(k, 1), :]
+    one, two, three = pieces(tile[...])
+    stacked = jnp.concatenate([one, two, three, jnp.zeros((8, SLOTS), F32)], axis=0).astype(BF16)
+    moved = lax.dot_general(stacked, order[...], (((1,), (1,)), ((), ())), preferred_element_type=F32)
+    moved = moved[0:8] + moved[8:16] + moved[16:24]
+    chosen[...] = jnp.full(chosen.shape, -1, jnp.int32)
+    for j in range(SLOTS // LANES):
+        chosen[pl.ds(j, 1), :] = moved[0:1, j * LANES : (j + 1) * LANES].astype(jnp.int32) - 1
+    nodes = chosen[...]
+    tile[pl.ds(3, 3), :] = moved[1:4]
     for k in range(3):
         tables = [jnp.broadcast_to(ext_c[2 + s, pl.ds(k, 1), :], (8, LANES)) for s in range(8)]
-        spot = pick(tables, slot_ids)
+        where = pick(tables, nodes)
         for j in range(SLOTS // LANES):
-            mine[pl.ds(k, 1), pl.ds(j * LANES, LANES)] = spot[j : j + 1, :]
-        mine[pl.ds(3 + k, 1), pl.ds(0, count)] = an_ref[pl.ds(k, 1), :]
-    for j in range(SLOTS // LANES):
-        mine[pl.ds(6, 1), pl.ds(j * LANES, LANES)] = live[j : j + 1, :]
-
-    pl.semaphore_wait(barrier, len(others) + 2)
+            tile[pl.ds(k, 1), pl.ds(j * LANES, LANES)] = where[j : j + 1, :]
+    near[row] = tile[:, 0:WIDE]
+
+    pl.semaphore_wait(barrier, len(greeted) + 8 * at_end.astype(jnp.int32))
     coords_sent = halo(ext_c, 0)
-    static_sent = gather_stage(g_ref, 0, 0)
+    static_sent = share(source, 0)
+    mine = near.at[row]
+    column_sent = [send(mine, mine, near_s.at[j], near_r.at[j], column[j]) for j in range(7)]
+
+    @pl.when(at_end)
+    def _():
+        for r in range(8):
+            remote(tile.at[:, pl.ds(WIDE, WIDE)], far, far_s.at[r], far_r, helpers[r]).start()
 
     full = elems // LANES
     for a in range(4):
@@ -198,8 +256,6 @@
         return total[0:8] + total[8:16] + total[16:24]
 
     finish(coords_sent)
-    finish(static_sent)
-    static_sent = gather_stage(g_ref, 0, 1)
 
     def shape_elements(i, carry):
         at = pl.ds(pl.multiple_of(i * 8, 8), 8)
@@ -231,10 +287,10 @@
         return carry
 
     lax.fori_loop(0, tet_rows // 8, shape_elements, 0)
+    finish(static_sent)
+    static_sent = share_on(source, 0)
     reaction = rea_ref[...]
     diagonal = reaction + node_sums()
-    finish(static_sent)
-    static_sent = gather_stage(g_ref, 0, 2)
 
     resid = load_ref[...]
     x = direction = image = gamma_old = alpha = None
@@ -279,85 +335,140 @@
 
     sol_ref[...] = x
     tables = [jnp.broadcast_to(x[s : s + 1, :], (8, LANES)) for s in range(8)]
-    t_ref[z_hi, y, z_lo, g] = pick(tables, slot_ids)
+    trace[col] = pick(tables, nodes)
+    trace_sent = share(trace, 1)
+    own_trace = pick(tables, slot_ids)
+
+    def split_target(b, tile, first):
+        t = tile[0:3] - first
+        t_one, t_two, t_three = pieces(t)
+        q_one, q_two, q_three = pieces(dot3((t[0:1], t[1:2], t[2:3]), (t[0:1], t[1:2], t[2:3])))
+        none3, none1 = jnp.zeros((3, WIDE), F32), jnp.zeros((1, WIDE), F32)
+        unit = jnp.ones((1, WIDE), F32)
+        blocks_d, blocks_n = [], []
+        for piece, lead in ((t_one, 1), (t_two, 0), (t_three, 0), (t_one, 1), (t_two, 0), (t_one, 1)):
+            flag = unit if lead else none1
+            blocks_d += [-2.0 * piece, none3, flag, none1]
+            blocks_n += [none3, piece, none1, -flag]
+        blocks_d += [q_one, q_two, q_three] + [none1] * 13
+        blocks_n += [none1] * 16
+        fill = jnp.zeros((64, WIDE), F32)
+        for i, blocks in enumerate((blocks_d, blocks_n)):
+            lhs[b, i] = jnp.concatenate(blocks + [fill], axis=0).T[:, 0:64].astype(BF16)
+
     finish(static_sent)
-    for stage in range(3):
-        finish(gather_stage(t_ref, 1, stage))
-
-
-def pair_kernel(g_ref, t_ref, out_ref, lhs, acc, rows):
-    row, col = lax.axis_index("row"), lax.axis_index("col")
-    me = row * 16 + col
-    count = out_ref.shape[1]
-    padded = acc.shape[0]
-
-    def trace_row(p):
-        tile = t_ref[p]
-        return jnp.concatenate([tile[j : j + 1, :] for j in range(SLOTS // LANES)], axis=1)
-
-    own = g_ref[me]
-    first = jnp.max(jnp.where(own[6:7] > 0, 1.0, 0.0) * own[0:3] + jnp.where(own[6:7] > 0, 0.0, -1e9), axis=1, keepdims=True)
-    centre = jnp.concatenate([first, jnp.zeros((5, 1), F32)], axis=0)
-    t = own[0:3] - first
-    t_one, t_two, t_three = pieces(t)
-    q_one, q_two, q_three = pieces(dot3((t[0:1], t[1:2], t[2:3]), (t[0:1], t[1:2], t[2:3])))
-    none3 = jnp.zeros((3, SLOTS), F32)
-    none1 = jnp.zeros((1, SLOTS), F32)
-    unit = jnp.ones((1, SLOTS), F32)
-    blocks_d, blocks_n = [], []
-    for part, lead in ((t_one, 1), (t_two, 0), (t_three, 0), (t_one, 1), (t_two, 0), (t_one, 1)):
-        flag = unit if lead else none1
-        blocks_d += [-2.0 * part, none3, flag, none1]
-        blocks_n += [none3, part, none1, -flag]
-    blocks_d += [q_one, q_two, q_three] + [none1] * 13
-    blocks_n += [none1] * 16
-    fill = jnp.zeros((64, SLOTS), F32)
-    for i, blocks in enumerate((blocks_d, blocks_n)):
-        stacked = jnp.concatenate(blocks + [fill], axis=0)
-        lhs[i] = stacked.T[0:padded, 0:64].astype(BF16)
-    acc[...] = jnp.zeros_like(acc)
-    rows[...] = jnp.zeros_like(rows)
-    rows[pl.ds(48, 8), :] = jnp.where(lax.broadcasted_iota(jnp.int32, (8, SLOTS), 0) < 3, 1.0, 0.0).astype(F32)
-
-    def step(p, carry):
-        tile = g_ref[p]
-        trace = trace_row(p)
-        s = tile[0:3] - first
-        w = tile[3:6] * trace
-        sx, wx = [s[k : k + 1] for k in range(3)], [w[k : k + 1] for k in range(3)]
-        data = jnp.concatenate([s, w, dot3(sx, sx) + 0.25, dot3(sx, wx)], axis=0)
-        one, two, three = pieces(data)
-        for i, part in enumerate((one, one, one, two, two, three)):
-            rows[pl.ds(8 * i, 8), :] = part
-        rhs = rows[...].astype(BF16)
-        for m in range(0, padded, 64):
-            d = jnp.dot(lhs[0, m : m + 64, :], rhs, preferred_element_type=F32)
-            n = jnp.dot(lhs[1, m : m + 64, :], rhs, preferred_element_type=F32)
-            inv = lax.rsqrt(d)
-            c = (n * inv) * (inv * inv)
-            acc[m : m + 64, :] += (c[:, 0:128] + c[:, 128:256]) + (c[:, 256:384] + c[:, 384:512])
+    finish(column_sent)
+    remote(far, far, far_s.at[0], far_r, keeper).wait_recv()
+
+    @pl.when(at_end)
+    def _():
+        for r in range(8):
+            remote(tile.at[:, pl.ds(WIDE, WIDE)], far, far_s.at[r], far_r, helpers[r]).wait_send()
+
+    own_first = near[row][0:3, 0:1]
+    far_first = far[0:3, 0:1]
+
+    def split_near(b, carry):
+        split_target(b, near[b], own_first)
         return carry
 
-    lax.fori_loop(0, g_ref.shape[0], step, 0)
-    sums = jnp.sum(acc[...].T, axis=0, keepdims=True) * (0.25 / math.pi)
-    trace = trace_row(me)
-    result = own[6:7, 0:padded] * (-0.5 * trace[:, 0:padded] + sums)
-    out_ref[...] = result[:, 0:count]
+    lax.fori_loop(0, 8, split_near, 0)
+    split_target(8, far[...], far_first)
+
+    finish(trace_sent)
+    finish(share_on(trace, 1))
+
+    def split_sources(first):
+        unit = jnp.where(lax.broadcasted_iota(jnp.int32, (8, WIDE), 0) < 3, 1.0, 0.0).astype(F32)
+
+        def put(i, tile, tr):
+            s = tile[0:3] - first
+            w = tile[3:6] * tr
+            sx, wx = [s[k : k + 1] for k in range(3)], [w[k : k + 1] for k in range(3)]
+            data = jnp.concatenate([s, w, dot3(sx, sx) + 0.25, dot3(sx, wx)], axis=0)
+            one, two, three = pieces(data)
+            block = jnp.concatenate([one, one, one, two, two, three, unit, jnp.zeros((8, WIDE), F32)], axis=0)
+            rhs[:, pl.ds(pl.multiple_of(i * WIDE, WIDE), WIDE)] = block.astype(BF16)
+
+        def each(c, carry):
+            tr = trace[c]
+            put(c, source[c, :, pl.ds(0, WIDE)], jnp.concatenate([tr[0:1], tr[1:2]], axis=1))
+            return carry
+
+        lax.fori_loop(0, 16, each, 0)
+        for i, c in ((16, 0), (17, 15)):
+            tr = trace[c]
+            put(i, source[c, :, pl.ds(WIDE, WIDE)], jnp.concatenate([tr[2:3], tr[3:4]], axis=1))
+
+    def pair_sums(b):
+        parts = []
+        for low, high in ((0, 128), (128, BLOCK)):
+            left_d, left_n = lhs[b, 0, low:high, :], lhs[b, 1, low:high, :]
+
+            def some(i, total):
+                for u in range(UNROLL):
+                    right = rhs[:, pl.ds(pl.multiple_of((i * UNROLL + u) * WIDE, WIDE), WIDE)]
+                    d = jnp.dot(left_d, right, preferred_element_type=F32)
+                    n = jnp.dot(left_n, right, preferred_element_type=F32)
+                    inv = lax.rsqrt(d)
+                    c = (n * inv) * (inv * inv)
+                    total = total + (c[:, 0:LANES] + c[:, LANES:WIDE])
+                return total
+
+            parts.append(lax.fori_loop(0, 18 // UNROLL, some, jnp.zeros((high - low, LANES), F32)))
+        parts.append(jnp.zeros((WIDE - BLOCK, LANES), F32))
+        return jnp.sum(jnp.concatenate(parts, axis=0).T, axis=0, keepdims=True)
+
+    def keep(ref, sums):
+        ref[pl.ds(0, 1), :] = sums[:, 0:LANES]
+        ref[pl.ds(1, 1), :] = sums[:, LANES:WIDE]
+
+    split_sources(far_first)
+    keep(part.at[8], pair_sums(8))
+    fex_sent = send(part.at[8], fex.at[row], fex_s, fex_r.at[row], keeper)
+    split_sources(own_first)
+
+    def one_row(j, carry):
+        other = (row + j) % 8
+        keep(part.at[other], pair_sums(other))
+        remote(part.at[other], fin.at[row], fin_s.at[j - 1], fin_r.at[j - 1], (other, col)).start()
+        return carry
+
+    lax.fori_loop(1, 8, one_row, 0)
+    keep(part.at[row], pair_sums(row))
+    fin[row] = part[row]
+    fex_sent.wait_send()
+    for j in range(7):
+        remote(part.at[row], fin.at[row], fin_s.at[j], fin_r.at[j], column[j]).wait()
+
+    @pl.when(at_end)
+    def _():
+        for r in range(8):
+            remote(part.at[8], fex.at[r], fex_s, fex_r.at[r], keeper).wait_recv()
+
+    total, more = fin[0], fex[0]
+    for r in range(1, 8):
+        total, more = total + fin[r], more + fex[r]
+    tables = [jnp.broadcast_to(v[j : j + 1, :], (8, LANES)) for v in (total, more) for j in range(2)]
+    result = live * (-0.5 * own_trace + (0.25 / math.pi) * pick(tables, spot))
+    for j in range(SLOTS // LANES):
+        width = min(LANES, count - j * LANES)
+        out_ref[:, pl.ds(j * LANES, width)] = result[j : j + 1, 0:width]
 
 
 def local(node_coords, tet_nodes, bnd_nodes, reaction, load, area_normal):
     elems, count = tet_nodes.shape[1], bnd_nodes.shape[0]
     tet_rows = -(-elems // 1024) * 8
     length = 4 * tet_rows * LANES
-    sol, gathered, traces = pl.pallas_call(
-        chain_kernel,
+    dma = pltpu.SemaphoreType.DMA
+    sol, demag = pl.pallas_call(
+        full_kernel,
         out_shape=(
             jax.ShapeDtypeStruct((8, LANES), F32),
-            jax.ShapeDtypeStruct((2, 4, 2, 8, 8, SLOTS), F32),
-            jax.ShapeDtypeStruct((2, 4, 2, 8, 8, LANES), F32),
+            jax.ShapeDtypeStruct((1, count), F32),
         ),
         in_specs=[VMEM] * 6,
-        out_specs=(VMEM,) * 3,
+        out_specs=(VMEM,) * 2,
         scratch_shapes=[
             pltpu.VMEM((4, tet_rows, LANES), jnp.int32),
             pltpu.VMEM((12, 8, LANES), F32),
@@ -367,34 +478,32 @@
             pltpu.VMEM((10, tet_rows, LANES), F32),
             pltpu.VMEM((4, tet_rows, LANES), F32),
             pltpu.VMEM((8, LANES), jnp.int32),
+            pltpu.VMEM((8, LANES), jnp.int32),
+            pltpu.VMEM((SLOTS, SLOTS), BF16),
+            pltpu.VMEM((16, 8, SLOTS), F32),
+            pltpu.VMEM((16, 8, LANES), F32),
+            pltpu.VMEM((8, 8, WIDE), F32),
+            pltpu.VMEM((8, WIDE), F32),
+            pltpu.VMEM((64, 18 * WIDE), BF16),
+            pltpu.VMEM((9, 2, WIDE, 64), BF16),
+            pltpu.VMEM((9, 8, LANES), F32),
+            pltpu.VMEM((8, 8, LANES), F32),
+            pltpu.VMEM((8, 8, LANES), F32),
             pltpu.VMEM((ITERS, 8, 2, 8, LANES), F32),
             pltpu.VMEM((ITERS, 4, 2, 8, LANES), F32),
             pltpu.VMEM((ITERS, 4, 2, 8, LANES), F32),
-            pltpu.SemaphoreType.DMA((1 + ITERS, 2)),
-            pltpu.SemaphoreType.DMA((1 + ITERS, 2)),
-            pltpu.SemaphoreType.DMA((ITERS, 13)),
-            pltpu.SemaphoreType.DMA((ITERS, 13)),
-            pltpu.SemaphoreType.DMA((2, 13)),
-            pltpu.SemaphoreType.DMA((2, 13)),
+            dma((1 + ITERS, 2)), dma((1 + ITERS, 2)),
+            dma((ITERS, 13)), dma((ITERS, 13)),
+            dma((2, 8)), dma((2, 8)),
+            dma((7,)), dma((7,)),
+            dma((8,)), dma(()),
+            dma((7,)), dma((7,)),
+            dma(()), dma((8,)),
         ],
         compiler_params=pltpu.CompilerParams(collective_id=0, has_side_effects=True, vmem_limit_bytes=60 << 20),
-        name="chain",
+        name="full",
     )(tet_nodes, node_coords, bnd_nodes.reshape(1, count), area_normal,
       reaction.reshape(8, LANES), load.reshape(8, LANES))
-    padded = -(-count // 64) * 64
-    demag = pl.pallas_call(
-        pair_kernel,
-        out_shape=jax.ShapeDtypeStruct((1, count), F32),
-        in_specs=[VMEM] * 2,
-        out_specs=VMEM,
-        scratch_shapes=[
-            pltpu.VMEM((2, padded, 64), BF16),
-            pltpu.VMEM((padded, LANES), F32),
-            pltpu.VMEM((64, SLOTS), F32),
-        ],
-        compiler_params=pltpu.CompilerParams(vmem_limit_bytes=60 << 20),
-        name="pairs",
-    )(gathered.reshape(128, 8, SLOTS), traces.reshape(128, 8, LANES))
     return sol.reshape(-1), demag.reshape(-1)
 
 

time: 158 us -> 110 us (0.70)
  Pallas kernels: 155 us -> 107 us
    pallas_call x2 -> x1, Pallas kernels: 155 us -> 107 us  [local(): pl.pallas_call(full_kernel, out_shape=(jax.ShapeDtypeStruct((8, LANES), F...]
where the time goes in v2:
time: 110 us; the launch traced here: 109 us
  Pallas kernels  107 us (97%)
  local copies, waits for them, and re-layouts  1.91 us (2%)
    pallas_call x1, Pallas kernels, local(): pl.pallas_call(full_kernel, out_shape=(jax.ShapeDtypeStruct((8, LANES), F...  107 us

profile of v2, /device:TPU:24, one launch (start us, length us, event | category | flops | bytes accessed | tf_op | source)
XLA Modules:
  0.0 109.4 jit_solution(6678805625963835848)
XLA Ops:
  0.6 106.8 %full.1 = (f32[8,128]{1,0:T(8,128)}, f32[1,436]{1,0:T(1,128)}) custom-call(s32[4,6750]{1,0:T(4,128)} %tet_ref.1, f32[3,1024]{1,0:T(4,128)} %nc_ref.1, s32[1,436]{1,0:T(1,128)} %bitcast.8, f32[3,436]{1,0:T(4,128)} %an_ref.1, f32[8,128]{1,0:T(8,128)} %bitcast.5, f32[8,128]{1,0:T(8,128)} %bitcast.6), custom_call_target="tpu_custom_call" | custom-call | tf_op jit(solution)/shard_map/full/pallas_call | solution.py:464
  107.5 0.0 copy-start
  107.5 0.7 copy-done
  108.1 0.0 copy-start.1
  108.1 0.6 copy.10
  108.7 0.1 copy-done.1
  108.8 0.6 copy.11
Async XLA Ops:
  107.5 0.7 copy-start
  108.1 0.7 copy-start.1

commit v3 on v2

--- a/solution.py
+++ b/solution.py
@@ -15,7 +15,7 @@
 BF16 = jnp.bfloat16
 MESH = pl.DeviceIdType.MESH
 VMEM = pl.BlockSpec(memory_space=pltpu.VMEM)
-CHUNK = 2048
+CHUNK = 7168
 QS = 16
 WIDE = 256
 MAIN = 4 * 4 * (QS - 1)
@@ -101,14 +101,9 @@
     part[...] = jnp.zeros(part.shape, F32)
 
     barrier = pltpu.get_barrier_semaphore()
-    greeted = others + column + [before, after, keeper]
+    greeted = others + [before, after]
     for who in greeted:
         pl.semaphore_signal(barrier, inc=1, device_id=who, device_id_type=MESH)
-
-    @pl.when(at_end)
-    def _():
-        for who in helpers:
-            pl.semaphore_signal(barrier, inc=1, device_id=who, device_id_type=MESH)
 
     def remote(src, dst, ssem, rsem, who):
         return pltpu.make_async_remote_copy(
@@ -139,20 +134,35 @@
         for copy in copies:
             copy.wait()
 
-    def reduce_all(u, v, k):
-        for buf, mine, size, first in ((red_a, g, 8, 0), (red_y, y, 4, 7), (red_z, z, 4, 10)):
-            here = buf.at[k]
-            here[mine, 0] = u
-            here[mine, 1] = v
-            tile = here.at[mine]
-            finish([
-                send(tile, tile, red_s.at[k, first + j], red_r.at[k, first + j], others[first + j])
-                for j in range(size - 1)
-            ])
-            u, v = here[0, 0], here[0, 1]
-            for i in range(1, size):
-                u, v = u + here[i, 0], v + here[i, 1]
-        return jnp.sum(u, keepdims=True), jnp.sum(v, keepdims=True)
+    groups = ((red_a, g, 8, 0), (red_y, y, 4, 7), (red_z, z, 4, 10))
+
+    def reduce_stage(rows, k, stage):
+        buf, mine, size, first = groups[stage]
+        buf[k, mine, pl.ds(0, 2), :] = rows
+        tile = buf.at[k, mine, pl.ds(0, 2)]
+        return [
+            send(tile, tile, red_s.at[k, first + j], red_r.at[k, first + j], others[first + j])
+            for j in range(size - 1)
+        ]
+
+    def reduce_sum(copies, k, stage):
+        finish(copies)
+        buf, _, size, _ = groups[stage]
+        rows = buf[k, 0, pl.ds(0, 2), :]
+        for i in range(1, size):
+            rows = rows + buf[k, i, pl.ds(0, 2), :]
+        return rows
+
+    def reduce_begin(u, v, k):
+        rows = jnp.concatenate([jnp.sum(u, axis=0, keepdims=True), jnp.sum(v, axis=0, keepdims=True)], axis=0)
+        return reduce_stage(rows, k, 0)
+
+    def reduce_on(copies, k, stage):
+        return reduce_stage(reduce_sum(copies, k, stage), k, stage + 1)
+
+    def reduce_end(copies, k):
+        rows = jnp.sum(reduce_sum(copies, k, 2), axis=1, keepdims=True)
+        return rows[0:1], rows[1:2]
 
     for s in range(8):
         for k in range(3):
@@ -203,16 +213,18 @@
             tile[pl.ds(k, 1), pl.ds(j * LANES, LANES)] = where[j : j + 1, :]
     near[row] = tile[:, 0:WIDE]
 
-    pl.semaphore_wait(barrier, len(greeted) + 8 * at_end.astype(jnp.int32))
+    pl.semaphore_wait(barrier, len(greeted))
     coords_sent = halo(ext_c, 0)
     static_sent = share(source, 0)
-    mine = near.at[row]
-    column_sent = [send(mine, mine, near_s.at[j], near_r.at[j], column[j]) for j in range(7)]
-
-    @pl.when(at_end)
-    def _():
-        for r in range(8):
-            remote(tile.at[:, pl.ds(WIDE, WIDE)], far, far_s.at[r], far_r, helpers[r]).start()
+
+    def send_targets():
+        for j in range(7):
+            send(near.at[row], near.at[row], near_s.at[j], near_r.at[j], column[j])
+
+        @pl.when(at_end)
+        def _():
+            for r in range(8):
+                remote(tile.at[:, pl.ds(WIDE, WIDE)], far, far_s.at[r], far_r, helpers[r]).start()
 
     full = elems // LANES
     for a in range(4):
@@ -234,7 +246,7 @@
 
     lax.fori_loop(0, tet_rows, build, 0)
 
-    def node_sums():
+    def node_sums(between=None):
         def spread_rows(q, carry):
             level = lax.broadcasted_iota(jnp.int32, (8, LANES), 0) + 2
             for a in range(4):
@@ -246,6 +258,8 @@
             return carry
 
         lax.fori_loop(0, tet_rows, spread_rows, 0)
+        if between is not None:
+            between()
 
         def accumulate(i, total):
             at = pl.ds(pl.multiple_of(i * CHUNK, CHUNK), CHUNK)
@@ -292,14 +306,13 @@
     reaction = rea_ref[...]
     diagonal = reaction + node_sums()
 
-    resid = load_ref[...]
-    x = direction = image = gamma_old = alpha = None
-    for k in range(ITERS):
+    def apply(field, k, running=None):
         table = ext_v.at[k]
-        precond = resid / diagonal
         for s in range(8):
-            table[2 + s] = jnp.broadcast_to(precond[s : s + 1, :], (8, LANES))
+            table[2 + s] = jnp.broadcast_to(field[s : s + 1, :], (8, LANES))
         finish(halo(table, 1 + k))
+        if running is not None:
+            running.append(reduce_on(running.pop(), k - 1, 0))
 
         def products(i, carry):
             at = pl.ds(pl.multiple_of(i * 8, 8), 8)
@@ -317,27 +330,43 @@
             return carry
 
         lax.fori_loop(0, tet_rows // 8, products, 0)
-        applied = reaction * precond + node_sums()
-        gamma, delta = reduce_all(resid * precond, precond * applied, k)
+
+        def between():
+            if running is not None:
+                running.append(reduce_on(running.pop(), k - 1, 1))
+
+        return reaction * field + node_sums(between)
+
+    r = load_ref[...]
+    u = r / diagonal
+    w = apply(u, 0)
+    x = zz = q = s_ = p = gamma_old = alpha = None
+    for k in range(ITERS - 1):
+        running = [reduce_begin(r * u, w * u, k)]
+        m = w / diagonal
+        n = apply(m, k + 1, running)
+        gamma, delta = reduce_end(running.pop(), k)
         if k == 0:
             alpha = gamma / delta
-            direction, image = precond, applied
-            x = alpha * direction
+            zz, q, s_, p = n, m, w, u
+            x = alpha * p
         else:
             beta = gamma / gamma_old
             alpha = gamma / (delta - beta * gamma / alpha)
-            direction = precond + beta * direction
-            image = applied + beta * image
-            x = x + alpha * direction
-        if k + 1 < ITERS:
-            resid = resid - alpha * image
+            zz, q, s_, p = n + beta * zz, m + beta * q, w + beta * s_, u + beta * p
+            x = x + alpha * p
+        r, u, w = r - alpha * s_, u - alpha * q, w - alpha * zz
         gamma_old = gamma
-
-    sol_ref[...] = x
-    tables = [jnp.broadcast_to(x[s : s + 1, :], (8, LANES)) for s in range(8)]
-    trace[col] = pick(tables, nodes)
+        if k == 0:
+            send_targets()
+    last = ITERS - 1
+    running = reduce_begin(r * u, w * u, last)
+
+    for i, part_of in enumerate((x, u, p)):
+        tables = [jnp.broadcast_to(part_of[s : s + 1, :], (8, LANES)) for s in range(8)]
+        trace[col, pl.ds(4 * i, 4), :] = pick(tables, nodes)[0:4]
     trace_sent = share(trace, 1)
-    own_trace = pick(tables, slot_ids)
+    running = reduce_on(running, last, 0)
 
     def split_target(b, tile, first):
         t = tile[0:3] - first
@@ -357,7 +386,8 @@
             lhs[b, i] = jnp.concatenate(blocks + [fill], axis=0).T[:, 0:64].astype(BF16)
 
     finish(static_sent)
-    finish(column_sent)
+    for j in range(7):
+        remote(near.at[row], near.at[row], near_s.at[j], near_r.at[j], column[j]).wait()
     remote(far, far, far_s.at[0], far_r, keeper).wait_recv()
 
     @pl.when(at_end)
@@ -376,7 +406,19 @@
     split_target(8, far[...], far_first)
 
     finish(trace_sent)
-    finish(share_on(trace, 1))
+    trace_sent = share_on(trace, 1)
+    running = reduce_on(running, last, 1)
+    gamma, delta = reduce_end(running, last)
+    beta = gamma / gamma_old
+    alpha = gamma / (delta - beta * gamma / alpha)
+    x = x + alpha * (u + beta * p)
+    sol_ref[...] = x
+    tables = [jnp.broadcast_to(x[s : s + 1, :], (8, LANES)) for s in range(8)]
+    own_trace = pick(tables, slot_ids)
+    finish(trace_sent)
+
+    def whole_trace(c):
+        return trace[c, pl.ds(0, 4), :] + alpha * (trace[c, pl.ds(4, 4), :] + beta * trace[c, pl.ds(8, 4), :])
 
     def split_sources(first):
         unit = jnp.where(lax.broadcasted_iota(jnp.int32, (8, WIDE), 0) < 3, 1.0, 0.0).astype(F32)
@@ -391,13 +433,13 @@
             rhs[:, pl.ds(pl.multiple_of(i * WIDE, WIDE), WIDE)] = block.astype(BF16)
 
         def each(c, carry):
-            tr = trace[c]
+            tr = whole_trace(c)
             put(c, source[c, :, pl.ds(0, WIDE)], jnp.concatenate([tr[0:1], tr[1:2]], axis=1))
             return carry
 
         lax.fori_loop(0, 16, each, 0)
         for i, c in ((16, 0), (17, 15)):
-            tr = trace[c]
+            tr = whole_trace(c)
             put(i, source[c, :, pl.ds(WIDE, WIDE)], jnp.concatenate([tr[2:3], tr[3:4]], axis=1))
 
     def pair_sums(b):
@@ -481,7 +523,7 @@
             pltpu.VMEM((8, LANES), jnp.int32),
             pltpu.VMEM((SLOTS, SLOTS), BF16),
             pltpu.VMEM((16, 8, SLOTS), F32),
-            pltpu.VMEM((16, 8, LANES), F32),
+            pltpu.VMEM((16, 16, LANES), F32),
             pltpu.VMEM((8, 8, WIDE), F32),
             pltpu.VMEM((8, WIDE), F32),
             pltpu.VMEM((64, 18 * WIDE), BF16),
@@ -489,9 +531,9 @@
             pltpu.VMEM((9, 8, LANES), F32),
             pltpu.VMEM((8, 8, LANES), F32),
             pltpu.VMEM((8, 8, LANES), F32),
-            pltpu.VMEM((ITERS, 8, 2, 8, LANES), F32),
-            pltpu.VMEM((ITERS, 4, 2, 8, LANES), F32),
-            pltpu.VMEM((ITERS, 4, 2, 8, LANES), F32),
+            pltpu.VMEM((ITERS, 8, 8, LANES), F32),
+            pltpu.VMEM((ITERS, 4, 8, LANES), F32),
+            pltpu.VMEM((ITERS, 4, 8, LANES), F32),
             dma((1 + ITERS, 2)), dma((1 + ITERS, 2)),
             dma((ITERS, 13)), dma((ITERS, 13)),
             dma((2, 8)), dma((2, 8)),

time: 110 us -> 82.4 us (0.75)
  Pallas kernels: 107 us -> 79.7 us
    pallas_call x1, Pallas kernels: 107 us -> 79.7 us  [local(): pl.pallas_call(full_kernel, out_shape=(jax.ShapeDtypeStruct((8, LANES), F...]
where the time goes in v3:
time: 82.4 us; the launch traced here: 82.2 us
  Pallas kernels  79.7 us (97%)
  local copies, waits for them, and re-layouts  1.91 us (2%)
    pallas_call x1, Pallas kernels, local(): pl.pallas_call(full_kernel, out_shape=(jax.ShapeDtypeStruct((8, LANES), F...  79.7 us
    unnamed x6, local copies, waits for them, and re-layouts  1.91 us

profile of v3, /device:TPU:24, one launch (start us, length us, event | category | flops | bytes accessed | tf_op | source)
XLA Modules:
  0.0 82.2 jit_solution(6483209102159840704)
XLA Ops:
  0.6 79.7 %full.1 = (f32[8,128]{1,0:T(8,128)}, f32[1,436]{1,0:T(1,128)}) custom-call(s32[4,6750]{1,0:T(4,128)} %tet_ref.1, f32[3,1024]{1,0:T(4,128)} %nc_ref.1, s32[1,436]{1,0:T(1,128)} %bitcast.8, f32[3,436]{1,0:T(4,128)} %an_ref.1, f32[8,128]{1,0:T(8,128)} %bitcast.5, f32[8,128]{1,0:T(8,128)} %bitcast.6), custom_call_target="tpu_custom_call" | custom-call | tf_op jit(solution)/shard_map/full/pallas_call | solution.py:506
  80.3 0.0 copy-start
  80.3 0.7 copy-done
  81.0 0.0 copy-start.1
  81.0 0.6 copy.10
  81.6 0.1 copy-done.1
  81.6 0.6 copy.11
Async XLA Ops:
  80.3 0.7 copy-start
  81.0 0.7 copy-start.1

commit v4 on v3

--- a/solution.py
+++ b/solution.py
@@ -18,9 +18,10 @@
 CHUNK = 7168
 QS = 16
 WIDE = 256
+HALF = 64
 MAIN = 4 * 4 * (QS - 1)
 BLOCK = 240
-UNROLL = 6
+UNROLL = 18
 PAIRS = [(a, b) for a in range(4) for b in range(a, 4)]
 
 
@@ -77,7 +78,7 @@
 def full_kernel(
     tet_ref, nc_ref, bnd_ref, an_ref, rea_ref, load_ref,
     sol_ref, out_ref,
-    ids, ext_c, ext_v, onehot, spread, stiff, vals, slots, chosen, order,
+    ids, ext_c, ext_v, onehot, spread, folded, stiff, vals, slots, chosen, order,
     source, trace, near, far, rhs, lhs, part, fin, fex,
     red_a, red_y, red_z,
     halo_s, halo_r, red_s, red_r, all_s, all_r, near_s, near_r, far_s, far_r,
@@ -98,6 +99,7 @@
     tet_rows = ids.shape[1]
 
     fex[...] = jnp.zeros(fex.shape, F32)
+    folded[...] = jnp.zeros(folded.shape, F32)
     part[...] = jnp.zeros(part.shape, F32)
 
     barrier = pltpu.get_barrier_semaphore()
@@ -237,9 +239,9 @@
             ids[a, pl.ds(full, 1), pl.ds(0, rest)] = tet_ref[pl.ds(a, 1), pl.ds(full * LANES, rest)]
 
     def build(q, carry):
-        lane = lax.broadcasted_iota(jnp.int32, (LANES, LANES), 0)
+        lane = lax.broadcasted_iota(jnp.int32, (HALF, LANES), 0)
         for a in range(4):
-            low = jnp.broadcast_to(ids[a, pl.ds(q, 1), :] & (LANES - 1), (LANES, LANES))
+            low = jnp.broadcast_to(ids[a, pl.ds(q, 1), :] & (HALF - 1), (HALF, LANES))
             hot = jnp.where(low == lane, 1.0, 0.0).astype(BF16)
             onehot[:, pl.ds(pl.multiple_of((q * 4 + a) * LANES, LANES), LANES)] = hot
         return carry
@@ -248,16 +250,19 @@
 
     def node_sums(between=None):
         def spread_rows(q, carry):
-            level = lax.broadcasted_iota(jnp.int32, (8, LANES), 0) + 2
+            level = lax.broadcasted_iota(jnp.int32, (16, LANES), 0) + 4
             for a in range(4):
-                high = jnp.broadcast_to(ids[a, pl.ds(q, 1), :] >> 7, (8, LANES))
+                high = jnp.broadcast_to(ids[a, pl.ds(q, 1), :] >> 6, (16, LANES))
                 val = jnp.broadcast_to(vals[a, pl.ds(q, 1), :], (8, LANES))
-                one, two, three = pieces(jnp.where(high == level, val, 0.0))
-                block = jnp.concatenate([one, two, three, jnp.zeros((8, LANES), F32)], axis=0)
+                one = val.astype(BF16).astype(F32)
+                hit = high == level
+                two = val - one
+                one, two = [jnp.where(hit, jnp.concatenate([v, v], axis=0), 0.0) for v in (one, two)]
+                block = jnp.concatenate([one, two], axis=0)
                 spread[:, pl.ds(pl.multiple_of((q * 4 + a) * LANES, LANES), LANES)] = block.astype(BF16)
             return carry
 
-        lax.fori_loop(0, tet_rows, spread_rows, 0)
+        lax.fori_loop(0, tet_rows, spread_rows, 0, unroll=4)
         if between is not None:
             between()
 
@@ -266,8 +271,11 @@
             return total + lax.dot_general(
                 spread[:, at], onehot[:, at], (((1,), (1,)), ((), ())), preferred_element_type=F32)
 
-        total = lax.fori_loop(0, onehot.shape[1] // CHUNK, accumulate, jnp.zeros((32, LANES), F32))
-        return total[0:8] + total[8:16] + total[16:24]
+        total = lax.fori_loop(0, onehot.shape[1] // CHUNK, accumulate, jnp.zeros((32, HALF), F32))
+        folded[:, pl.ds(0, HALF)] = total[0:16] + total[16:32]
+        even = folded[pl.ds(0, 8, stride=2), :]
+        odd = pltpu.roll(folded[pl.ds(1, 8, stride=2), :], HALF, 1)
+        return jnp.where(lax.broadcasted_iota(jnp.int32, (8, LANES), 1) < HALF, even, odd)
 
     finish(coords_sent)
 
@@ -329,7 +337,7 @@
                 vals[a, at, :] = sums[a]
             return carry
 
-        lax.fori_loop(0, tet_rows // 8, products, 0)
+        lax.fori_loop(0, tet_rows // 8, products, 0, unroll=True)
 
         def between():
             if running is not None:
@@ -420,7 +428,7 @@
     def whole_trace(c):
         return trace[c, pl.ds(0, 4), :] + alpha * (trace[c, pl.ds(4, 4), :] + beta * trace[c, pl.ds(8, 4), :])
 
-    def split_sources(first):
+    def split_sources(kind, first):
         unit = jnp.where(lax.broadcasted_iota(jnp.int32, (8, WIDE), 0) < 3, 1.0, 0.0).astype(F32)
 
         def put(i, tile, tr):
@@ -430,7 +438,7 @@
             data = jnp.concatenate([s, w, dot3(sx, sx) + 0.25, dot3(sx, wx)], axis=0)
             one, two, three = pieces(data)
             block = jnp.concatenate([one, one, one, two, two, three, unit, jnp.zeros((8, WIDE), F32)], axis=0)
-            rhs[:, pl.ds(pl.multiple_of(i * WIDE, WIDE), WIDE)] = block.astype(BF16)
+            rhs[kind, :, pl.ds(pl.multiple_of(i * WIDE, WIDE), WIDE)] = block.astype(BF16)
 
         def each(c, carry):
             tr = whole_trace(c)
@@ -442,14 +450,14 @@
             tr = whole_trace(c)
             put(i, source[c, :, pl.ds(WIDE, WIDE)], jnp.concatenate([tr[2:3], tr[3:4]], axis=1))
 
-    def pair_sums(b):
+    def pair_sums(b, kind):
         parts = []
         for low, high in ((0, 128), (128, BLOCK)):
             left_d, left_n = lhs[b, 0, low:high, :], lhs[b, 1, low:high, :]
 
             def some(i, total):
                 for u in range(UNROLL):
-                    right = rhs[:, pl.ds(pl.multiple_of((i * UNROLL + u) * WIDE, WIDE), WIDE)]
+                    right = rhs[kind, :, pl.ds(pl.multiple_of((i * UNROLL + u) * WIDE, WIDE), WIDE)]
                     d = jnp.dot(left_d, right, preferred_element_type=F32)
                     n = jnp.dot(left_n, right, preferred_element_type=F32)
                     inv = lax.rsqrt(d)
@@ -465,21 +473,27 @@
         ref[pl.ds(0, 1), :] = sums[:, 0:LANES]
         ref[pl.ds(1, 1), :] = sums[:, LANES:WIDE]
 
-    split_sources(far_first)
-    keep(part.at[8], pair_sums(8))
-    fex_sent = send(part.at[8], fex.at[row], fex_s, fex_r.at[row], keeper)
-    split_sources(own_first)
-
-    def one_row(j, carry):
+    split_sources(0, far_first)
+    split_sources(1, own_first)
+
+    def one_block(j, carry):
         other = (row + j) % 8
-        keep(part.at[other], pair_sums(other))
-        remote(part.at[other], fin.at[row], fin_s.at[j - 1], fin_r.at[j - 1], (other, col)).start()
+        b = jnp.where(j == 0, 8, other)
+        keep(part.at[b], pair_sums(b, jnp.minimum(j, 1)))
+
+        @pl.when(j == 0)
+        def _():
+            remote(part.at[8], fex.at[row], fex_s, fex_r.at[row], keeper).start()
+
+        @pl.when(jnp.logical_and(j > 0, j < 8))
+        def _():
+            remote(part.at[other], fin.at[row], fin_s.at[j - 1], fin_r.at[j - 1], (other, col)).start()
+
         return carry
 
-    lax.fori_loop(1, 8, one_row, 0)
-    keep(part.at[row], pair_sums(row))
+    lax.fori_loop(0, 9, one_block, 0)
     fin[row] = part[row]
-    fex_sent.wait_send()
+    remote(part.at[8], fex.at[row], fex_s, fex_r.at[row], keeper).wait_send()
     for j in range(7):
         remote(part.at[row], fin.at[row], fin_s.at[j], fin_r.at[j], column[j]).wait()
 
@@ -515,8 +529,9 @@
             pltpu.VMEM((4, tet_rows, LANES), jnp.int32),
             pltpu.VMEM((12, 8, LANES), F32),
             pltpu.VMEM((ITERS, 12, 8, LANES), F32),
-            pltpu.VMEM((LANES, length), BF16),
+            pltpu.VMEM((HALF, length), BF16),
             pltpu.VMEM((32, length), BF16),
+            pltpu.VMEM((16, LANES), F32),
             pltpu.VMEM((10, tet_rows, LANES), F32),
             pltpu.VMEM((4, tet_rows, LANES), F32),
             pltpu.VMEM((8, LANES), jnp.int32),
@@ -526,7 +541,7 @@
             pltpu.VMEM((16, 16, LANES), F32),
             pltpu.VMEM((8, 8, WIDE), F32),
             pltpu.VMEM((8, WIDE), F32),
-            pltpu.VMEM((64, 18 * WIDE), BF16),
+            pltpu.VMEM((2, 64, 18 * WIDE), BF16),
             pltpu.VMEM((9, 2, WIDE, 64), BF16),
             pltpu.VMEM((9, 8, LANES), F32),
             pltpu.VMEM((8, 8, LANES), F32),

time: 82.4 us -> 71.9 us (0.87)
  Pallas kernels: 79.7 us -> 69.1 us
    pallas_call x1, Pallas kernels: 79.7 us -> 69.1 us  [local(): pl.pallas_call(full_kernel, out_shape=(jax.ShapeDtypeStruct((8, LANES), F...]
where the time goes in v4:
time: 71.9 us; the launch traced here: 71.7 us
  Pallas kernels  69.1 us (96%)
  local copies, waits for them, and re-layouts  1.91 us (3%)
    pallas_call x1, Pallas kernels, local(): pl.pallas_call(full_kernel, out_shape=(jax.ShapeDtypeStruct((8, LANES), F...  69.1 us
    unnamed x6, local copies, waits for them, and re-layouts  1.91 us

profile of v4, /device:TPU:24, one launch (start us, length us, event | category | flops | bytes accessed | tf_op | source)
XLA Modules:
  0.0 71.7 jit_solution(8631299437626625350)
XLA Ops:
  0.6 69.1 %full.1 = (f32[8,128]{1,0:T(8,128)}, f32[1,436]{1,0:T(1,128)}) custom-call(s32[4,6750]{1,0:T(4,128)} %tet_ref.1, f32[3,1024]{1,0:T(4,128)} %nc_ref.1, s32[1,436]{1,0:T(1,128)} %bitcast.8, f32[3,436]{1,0:T(4,128)} %an_ref.1, f32[8,128]{1,0:T(8,128)} %bitcast.5, f32[8,128]{1,0:T(8,128)} %bitcast.6), custom_call_target="tpu_custom_call" | custom-call | tf_op jit(solution)/shard_map/full/pallas_call | solution.py:520
  69.8 0.0 copy-start
  69.8 0.7 copy-done
  70.5 0.0 copy-start.1
  70.5 0.6 copy.10
  71.1 0.1 copy-done.1
  71.1 0.6 copy.11
Async XLA Ops:
  69.8 0.7 copy-start
  70.5 0.7 copy-start.1

commit v5 on v4

--- a/solution.py
+++ b/solution.py
@@ -35,11 +35,11 @@
 def peers():
     row, col, z_hi, y, z_lo, g = place()
     out = [(row, z_lo * 8 + (g + j) % 8) for j in range(1, 8)]
-    out += [(z_hi * 4 + (y + j) % 4, col) for j in range(1, 4)]
-    z = z_hi * 2 + z_lo
-    for j in range(1, 4):
-        other = (z + j) % 4
-        out.append(((other // 2) * 4 + y, (other % 2) * 8 + g))
+    plane = (z_hi * 2 + z_lo) * 4 + y
+    for j in range(1, 16):
+        other = (plane + j) % 16
+        z = other // 4
+        out.append(((z // 2) * 4 + other % 4, (z % 2) * 8 + g))
     return out
 
 
@@ -80,7 +80,7 @@
     sol_ref, out_ref,
     ids, ext_c, ext_v, onehot, spread, folded, stiff, vals, slots, chosen, order,
     source, trace, near, far, rhs, lhs, part, fin, fex,
-    red_a, red_y, red_z,
+    red_a, red_b,
     halo_s, halo_r, red_s, red_r, all_s, all_r, near_s, near_r, far_s, far_r,
     fin_s, fin_r, fex_s, fex_r,
 ):
@@ -124,19 +124,21 @@
             send(buf.at[pl.ds(8, 2)], buf.at[pl.ds(0, 2)], halo_s.at[k, 1], halo_r.at[k, 1], after),
         ]
 
+    shared = (8, 12)
+
     def share(buf, k):
-        tile = buf.at[col]
+        tile = buf.at[col, pl.ds(0, shared[k])]
         return [send(tile, tile, all_s.at[k, j], all_r.at[k, j], others[j]) for j in range(7)]
 
     def share_on(buf, k):
-        tiles = buf.at[pl.ds(z_lo * 8, 8)]
+        tiles = buf.at[pl.ds(z_lo * 8, 8), pl.ds(0, shared[k])]
         return [send(tiles, tiles, all_s.at[k, 7], all_r.at[k, 7], partner)]
 
     def finish(copies):
         for copy in copies:
             copy.wait()
 
-    groups = ((red_a, g, 8, 0), (red_y, y, 4, 7), (red_z, z, 4, 10))
+    groups = ((red_a, g, 8, 0), (red_b, z * 4 + y, 16, 7))
 
     def reduce_stage(rows, k, stage):
         buf, mine, size, first = groups[stage]
@@ -163,7 +165,7 @@
         return reduce_stage(reduce_sum(copies, k, stage), k, stage + 1)
 
     def reduce_end(copies, k):
-        rows = jnp.sum(reduce_sum(copies, k, 2), axis=1, keepdims=True)
+        rows = jnp.sum(reduce_sum(copies, k, 1), axis=1, keepdims=True)
         return rows[0:1], rows[1:2]
 
     for s in range(8):
@@ -248,7 +250,7 @@
 
     lax.fori_loop(0, tet_rows, build, 0)
 
-    def node_sums(between=None):
+    def node_sums():
         def spread_rows(q, carry):
             level = lax.broadcasted_iota(jnp.int32, (16, LANES), 0) + 4
             for a in range(4):
@@ -263,8 +265,6 @@
             return carry
 
         lax.fori_loop(0, tet_rows, spread_rows, 0, unroll=4)
-        if between is not None:
-            between()
 
         def accumulate(i, total):
             at = pl.ds(pl.multiple_of(i * CHUNK, CHUNK), CHUNK)
@@ -309,8 +309,6 @@
         return carry
 
     lax.fori_loop(0, tet_rows // 8, shape_elements, 0)
-    finish(static_sent)
-    static_sent = share_on(source, 0)
     reaction = rea_ref[...]
     diagonal = reaction + node_sums()
 
@@ -339,11 +337,7 @@
 
         lax.fori_loop(0, tet_rows // 8, products, 0, unroll=True)
 
-        def between():
-            if running is not None:
-                running.append(reduce_on(running.pop(), k - 1, 1))
-
-        return reaction * field + node_sums(between)
+        return reaction * field + node_sums()
 
     r = load_ref[...]
     u = r / diagonal
@@ -367,6 +361,8 @@
         gamma_old = gamma
         if k == 0:
             send_targets()
+            finish(static_sent)
+            static_sent = share_on(source, 0)
     last = ITERS - 1
     running = reduce_begin(r * u, w * u, last)
 
@@ -415,7 +411,6 @@
 
     finish(trace_sent)
     trace_sent = share_on(trace, 1)
-    running = reduce_on(running, last, 1)
     gamma, delta = reduce_end(running, last)
     beta = gamma / gamma_old
     alpha = gamma / (delta - beta * gamma / alpha)
@@ -452,7 +447,7 @@
 
     def pair_sums(b, kind):
         parts = []
-        for low, high in ((0, 128), (128, BLOCK)):
+        for low, high in ((0, BLOCK),):
             left_d, left_n = lhs[b, 0, low:high, :], lhs[b, 1, low:high, :]
 
             def some(i, total):
@@ -547,10 +542,9 @@
             pltpu.VMEM((8, 8, LANES), F32),
             pltpu.VMEM((8, 8, LANES), F32),
             pltpu.VMEM((ITERS, 8, 8, LANES), F32),
-            pltpu.VMEM((ITERS, 4, 8, LANES), F32),
-            pltpu.VMEM((ITERS, 4, 8, LANES), F32),
+            pltpu.VMEM((ITERS, 16, 8, LANES), F32),
             dma((1 + ITERS, 2)), dma((1 + ITERS, 2)),
-            dma((ITERS, 13)), dma((ITERS, 13)),
+            dma((ITERS, 22)), dma((ITERS, 22)),
             dma((2, 8)), dma((2, 8)),
             dma((7,)), dma((7,)),
             dma((8,)), dma(()),

time: 71.9 us -> 67.1 us (0.933)
  Pallas kernels: 69.1 us -> 64.3 us
    pallas_call x1, Pallas kernels: 69.1 us -> 64.3 us  [local(): pl.pallas_call(full_kernel, out_shape=(jax.ShapeDtypeStruct((8, LANES), F...]
where the time goes in v5:
time: 67.1 us; the launch traced here: 66.9 us
  Pallas kernels  64.3 us (96%)
  local copies, waits for them, and re-layouts  1.91 us (3%)
    pallas_call x1, Pallas kernels, local(): pl.pallas_call(full_kernel, out_shape=(jax.ShapeDtypeStruct((8, LANES), F...  64.3 us
    unnamed x6, local copies, waits for them, and re-layouts  1.91 us

profile of v5, /device:TPU:24, one launch (start us, length us, event | category | flops | bytes accessed | tf_op | source)
XLA Modules:
  0.0 66.9 jit_solution(16917800448946723716)
XLA Ops:
  0.6 64.3 %full.1 = (f32[8,128]{1,0:T(8,128)}, f32[1,436]{1,0:T(1,128)}) custom-call(s32[4,6750]{1,0:T(4,128)} %tet_ref.1, f32[3,1024]{1,0:T(4,128)} %nc_ref.1, s32[1,436]{1,0:T(1,128)} %bitcast.8, f32[3,436]{1,0:T(4,128)} %an_ref.1, f32[8,128]{1,0:T(8,128)} %bitcast.5, f32[8,128]{1,0:T(8,128)} %bitcast.6), custom_call_target="tpu_custom_call" | custom-call | tf_op jit(solution)/shard_map/full/pallas_call | solution.py:515
  64.9 0.0 copy-start
  65.0 0.7 %copy-done = f32[8,128]{1,0:T(8,128)S(1)} copy-done((f32[8,128]{1,0:T(8,128)S(1)}, f32[8,128]{1,0:T(8,128)}, u32[]{:S(2)}) %copy-start) | copy-done | bytes 4120
  65.6 0.0 copy-start.1
  65.6 0.6 copy.10
  66.2 0.1 copy-done.1
  66.3 0.6 copy.11
Async XLA Ops:
  64.9 0.7 %copy-start = (f32[8,128]{1,0:T(8,128)S(1)}, f32[8,128]{1,0:T(8,128)}, u32[]{:S(2)}) copy-start(f32[8,128]{1,0:T(8,128)} %get-tuple-element.4) | copy-start | bytes 12292
  65.6 0.7 copy-start.1

commit v6 on v5

--- a/solution.py
+++ b/solution.py
@@ -146,7 +146,7 @@
         tile = buf.at[k, mine, pl.ds(0, 2)]
         return [
             send(tile, tile, red_s.at[k, first + j], red_r.at[k, first + j], others[first + j])
-            for j in range(size - 1)
+            for j in sorted(range(size - 1), key=lambda j: abs(2 * j - size))
         ]
 
     def reduce_sum(copies, k, stage):
@@ -316,9 +316,10 @@
         table = ext_v.at[k]
         for s in range(8):
             table[2 + s] = jnp.broadcast_to(field[s : s + 1, :], (8, LANES))
-        finish(halo(table, 1 + k))
+        sent = halo(table, 1 + k)
         if running is not None:
             running.append(reduce_on(running.pop(), k - 1, 0))
+        finish(sent)
 
         def products(i, carry):
             at = pl.ds(pl.multiple_of(i * 8, 8), 8)

time: 67.1 us -> 66.8 us (level)
  no operation moved by 1% of the time
where the time goes in v6:
time: 66.8 us; the launch traced here: 66.7 us
  Pallas kernels  64.1 us (96%)
  local copies, waits for them, and re-layouts  1.91 us (3%)
    pallas_call x1, Pallas kernels, local(): pl.pallas_call(full_kernel, out_shape=(jax.ShapeDtypeStruct((8, LANES), F...  64.1 us
    unnamed x6, local copies, waits for them, and re-layouts  1.91 us

profile of v6, /device:TPU:24, one launch (start us, length us, event | category | flops | bytes accessed | tf_op | source)
XLA Modules:
  0.0 66.7 jit_solution(7126701152525370840)
XLA Ops:
  0.6 64.1 %full.1 = (f32[8,128]{1,0:T(8,128)}, f32[1,436]{1,0:T(1,128)}) custom-call(s32[4,6750]{1,0:T(4,128)} %tet_ref.1, f32[3,1024]{1,0:T(4,128)} %nc_ref.1, s32[1,436]{1,0:T(1,128)} %bitcast.8, f32[3,436]{1,0:T(4,128)} %an_ref.1, f32[8,128]{1,0:T(8,128)} %bitcast.5, f32[8,128]{1,0:T(8,128)} %bitcast.6), custom_call_target="tpu_custom_call" | custom-call | tf_op jit(solution)/shard_map/full/pallas_call | solution.py:516
  64.7 0.0 copy-start
  64.7 0.7 %copy-done = f32[8,128]{1,0:T(8,128)S(1)} copy-done((f32[8,128]{1,0:T(8,128)S(1)}, f32[8,128]{1,0:T(8,128)}, u32[]{:S(2)}) %copy-start) | copy-done | bytes 4120
  65.4 0.0 copy-start.1
  65.4 0.6 copy.10
  66.0 0.1 copy-done.1
  66.1 0.6 copy.11
Async XLA Ops:
  64.7 0.7 %copy-start = (f32[8,128]{1,0:T(8,128)S(1)}, f32[8,128]{1,0:T(8,128)}, u32[]{:S(2)}) copy-start(f32[8,128]{1,0:T(8,128)} %get-tuple-element.4) | copy-start | bytes 12292
  65.4 0.7 copy-start.1
